TPU v7x, 256 devices: a whole 4x4x8 slice. The times are simulated.
256 devices in a mesh: sub: 2 (over x_lo), row: 8 (over y, x_hi), col: 16 (over z, core).
Axes of the slice: x: 4 (x_hi: 2, x_lo: 2; x = x_hi * 2 + x_lo), y: 4, z: 8, core: 2. Of those that a mesh axis runs over, the one named last changes fastest.
Arguments:
- front: float32 [10240, 10240], P(('sub', 'row'), 'col')
- children: float32 [4, 6144, 6144], P('sub', 'row', 'col')
- child_maps: int32 [4, 48], replicated, may hold values from 0 to 79, as said below
Outputs:
- factored: float32 [10240, 10240], P(('sub', 'row'), 'col')
Inputs may be any that keep to these rules, and one draw needn't show every extreme that they name: `child_maps`: each row holds 48 different parent block numbers, and entry i leaves the same remainder as i on division by 16. Child 0 sends its block 0 to parent block 0, child 1 its last block to parent block 79.
All inputs are finite; a program needn't handle non-finite values.
Results may differ from a plain program's by a relative error of at most 0.0001.
Values sent between devices are 32-bit elements; how exact they have to be, the bound alone decides.
A program may use at most 64 MiB of HBM per device.

v0:
```python
import jax
import jax.numpy as jnp
from jax import lax
from jax.sharding import PartitionSpec as P

BS = 128
NPB = 3


def from_root(value, axis, source):
    kept = jnp.where(lax.axis_index(axis) == source, value, 0).astype(value.dtype)
    return lax.psum(kept, axis)


def body(front, children, child_maps):
    n_sub = lax.axis_size("sub")
    n_row = lax.axis_size("row")
    n_col = lax.axis_size("col")
    rowdev = n_sub * n_row
    sub_idx = lax.axis_index("sub")
    row_idx = lax.axis_index("row")
    col_idx = lax.axis_index("col")
    dev_row = sub_idx * n_row + row_idx
    local_rows, local_cols = front.shape
    row_blocks = local_rows // BS
    col_blocks = local_cols // BS
    per_group, child_rows, child_cols = children.shape
    half_rows = child_rows // BS // n_sub
    child_cblocks = child_cols // BS
    highest = lax.Precision.HIGHEST
    col_pick = jnp.arange(child_cblocks, dtype=jnp.int32) * n_col + col_idx
    pieces = children.reshape(per_group, half_rows, n_sub, BS, child_cols)
    arrived = lax.all_to_all(pieces, "sub", split_axis=2, concat_axis=0, tiled=True)
    arrived = arrived.reshape(per_group * n_sub, half_rows, BS, child_cblocks, BS)
    row_pick = (jnp.arange(half_rows, dtype=jnp.int32) * n_sub + sub_idx) * n_row + row_idx
    row_dest = child_maps[:, row_pick] // rowdev
    col_dest = child_maps[:, col_pick] // n_col
    row_hot = (row_dest[..., None] == jnp.arange(row_blocks, dtype=jnp.int32)).astype(jnp.float32)
    col_hot = (col_dest[..., None] == jnp.arange(col_blocks, dtype=jnp.int32)).astype(jnp.float32)
    placed = jnp.einsum("cua,cuxmy->caxmy", row_hot, arrived, precision=highest)
    extended = jnp.einsum("caxmy,cmb->axby", placed, col_hot, precision=highest)
    assembled = front + extended.reshape(local_rows, local_cols)
    row_block = jnp.arange(local_rows, dtype=jnp.int32) // BS * rowdev + dev_row
    col_block = jnp.arange(local_cols, dtype=jnp.int32) // BS * n_col + col_idx
    col_ratio = n_col // rowdev
    identity = jnp.eye(BS, dtype=jnp.float32)

    def eliminate(section, matrix):
        section = section.astype(jnp.int32)
        owner_row = section % rowdev
        local_row = section // rowdev
        owner_col = section % n_col
        local_col = section // n_col
        corner = lax.dynamic_slice(matrix, (local_row * BS, local_col * BS), (BS, BS))
        diag_block = from_root(corner, ("sub", "row", "col"), owner_row * n_col + owner_col)
        factor = jnp.linalg.cholesky(diag_block)
        inverse = jax.scipy.linalg.solve_triangular(factor, identity, lower=True)
        column = lax.dynamic_slice_in_dim(matrix, local_col * BS, BS, 1)
        column_in = from_root(column, "col", owner_col)
        panel_rows = jnp.dot(column_in, inverse.T, precision=highest)
        below_mask = (row_block > section)[:, None]
        left_factor = jnp.where(below_mask, panel_rows, 0.0)
        right_mask = col_block > section
        grouped = panel_rows.reshape(col_blocks, col_ratio, BS, BS)
        chosen = lax.dynamic_index_in_dim(grouped, col_idx // rowdev, 1, keepdims=False)
        partner = from_root(chosen, ("sub", "row"), col_idx % rowdev)
        partner = jnp.where(right_mask.reshape(col_blocks, BS)[:, :, None], partner, 0.0)
        update = lax.dot_general(
            left_factor,
            partner.reshape(local_cols, BS),
            (((1,), (1,)), ((), ())),
            precision=highest,
        )
        matrix = matrix - update
        lower_tile = jnp.tile(jnp.tril(factor), (row_blocks, 1))
        written = jnp.where(
            below_mask, panel_rows, jnp.where((row_block == section)[:, None], lower_tile, 0.0)
        )
        current = lax.dynamic_slice_in_dim(matrix, local_col * BS, BS, 1)
        matrix = lax.dynamic_update_slice_in_dim(
            matrix, jnp.where(col_idx == owner_col, written, current), local_col * BS, 1
        )
        strip_now = lax.dynamic_slice_in_dim(matrix, local_row * BS, BS, 0)
        cleared = jnp.where((dev_row == owner_row) & right_mask[None, :], 0.0, strip_now)
        return lax.dynamic_update_slice_in_dim(matrix, cleared, local_row * BS, 0)

    return lax.fori_loop(0, NPB, eliminate, assembled)


def solution(mesh):
    return jax.shard_map(
        body,
        mesh=mesh,
        in_specs=(P(("sub", "row"), "col"), P("sub", "row", "col"), P()),
        out_specs=P(("sub", "row"), "col"),
        check_vma=False,
    )
```

profile of v0, /device:TPU:160, one launch (start us, length us, event | category | flops | bytes accessed | tf_op | source)
XLA Modules:
  0.0 1431.2 jit_solution(5333584483358286880)
XLA Ops:
  6.5 3.2 copy.23
  9.8 3.9 all-to-all-start
  15.1 26.5 %all-to-all-done = f32[2,3,2,128,384]{4,3,1,0,2:T(8,128)S(1)} async-done(((f32[2,3,2,128,384]{4,3,1,0,2:T(8,128)}), f32[2,3,2,128,384]{4,3,1,0,2:T(8,128)S(1)}, u32[]{:S(2)}, u32[]{:S(2)}) %all-to-all-start) | async-done | bytes 2359328 | tf_op jit(solution)/shard_map/all_to_all | solution.py:33
  41.6 2.0 copy.24
  43.6 3.2 copy.25
  46.8 4.0 fusion.30
  50.8 6.3 fusion.27
  57.6 1365.9 %while.17 = (s32[]{:T(128)}, f32[640,640]{1,0:T(8,128)S(1)}, s32[]{:T(128)}, s32[]{:T(128)}, s32[]{:T(128)}, /*index=5*/s32[]{:T(128)}, u32[]{:T(128)}, u32[]{:T...) while((s32[]{:T(128)}, f32[640,640]{1,0:T(8,128)S(1)}, ...), condition=%wide.region_6.7_spmd.clone.clone, body=%wide.region_0.6_spmd.clone.clone.sunk | while | flops 781671040 | bytes 13246939 | solution.py:87
  57.9 0.6 dynamic-slice_select_fusion.5
  58.6 0.8 dynamic-slice_select_fusion.4
  59.5 242.0 %all-reduce.6.cloned.1.call-done = f32[128,128]{1,0:T(8,128)} async-done(((f32[128,128]{1,0:T(8,128)}), f32[128,128]{1,0:T(8,128)}) %all-reduce.6.cloned.1.call-update) | async-done | bytes 65552 | tf_op jit(solution)/shard_map/while/body/eval_jaxpr/psum | solution.py:12
  301.4 0.9 copy.35
  302.4 0.9 fusion.67
  303.2 11.7 cholesky.85
  315.0 0.7 compare_reduce_fusion.2
  316.3 9.8 custom-call.28
  326.4 84.0 %all-reduce.4.cloned.1.call-done = f32[640,128]{1,0:T(8,128)} async-done(((f32[640,128]{1,0:T(8,128)}), f32[640,128]{1,0:T(8,128)}) %all-reduce.4.cloned.1.call-update) | async-done | bytes 327696 | tf_op jit(solution)/shard_map/while/body/eval_jaxpr/psum | solution.py:12
  410.4 2.1 broadcast_select_fusion.4
  413.3 97.5 %all-reduce.8.cloned.1.call-done = f32[5,128,128]{2,1,0:T(8,128)} async-done(((f32[5,128,128]{2,1,0:T(8,128)}), f32[5,128,128]{2,1,0:T(8,128)}) %all-reduce.8.cloned.1.call-update) | async-done | bytes 327696 | tf_op jit(solution)/shard_map/while/body/eval_jaxpr/psum | solution.py:12
  510.7 1.1 broadcast_select_fusion.5
  511.8 2.0 convolution_subtract_fusion.2
  514.3 0.6 dynamic-slice_select_fusion.5
  515.0 0.8 dynamic-slice_select_fusion.4
  515.9 240.2 %all-reduce.6.cloned.1.call-done = f32[128,128]{1,0:T(8,128)} async-done(((f32[128,128]{1,0:T(8,128)}), f32[128,128]{1,0:T(8,128)}) %all-reduce.6.cloned.1.call-update) | async-done | bytes 65552 | tf_op jit(solution)/shard_map/while/body/eval_jaxpr/psum | solution.py:12
  756.1 0.9 copy.35
  757.0 0.9 fusion.67
  757.9 11.7 cholesky.85
  769.6 0.7 compare_reduce_fusion.2
  770.9 9.8 custom-call.28
  781.1 83.8 %all-reduce.4.cloned.1.call-done = f32[640,128]{1,0:T(8,128)} async-done(((f32[640,128]{1,0:T(8,128)}), f32[640,128]{1,0:T(8,128)}) %all-reduce.4.cloned.1.call-update) | async-done | bytes 327696 | tf_op jit(solution)/shard_map/while/body/eval_jaxpr/psum | solution.py:12
  864.9 2.1 broadcast_select_fusion.4
  867.7 97.3 %all-reduce.8.cloned.1.call-done = f32[5,128,128]{2,1,0:T(8,128)} async-done(((f32[5,128,128]{2,1,0:T(8,128)}), f32[5,128,128]{2,1,0:T(8,128)}) %all-reduce.8.cloned.1.call-update) | async-done | bytes 327696 | tf_op jit(solution)/shard_map/while/body/eval_jaxpr/psum | solution.py:12
  965.0 1.1 broadcast_select_fusion.5
  966.2 2.0 convolution_subtract_fusion.2
  968.6 0.6 dynamic-slice_select_fusion.5
  969.3 0.8 dynamic-slice_select_fusion.4
  970.2 240.5 %all-reduce.6.cloned.1.call-done = f32[128,128]{1,0:T(8,128)} async-done(((f32[128,128]{1,0:T(8,128)}), f32[128,128]{1,0:T(8,128)}) %all-reduce.6.cloned.1.call-update) | async-done | bytes 65552 | tf_op jit(solution)/shard_map/while/body/eval_jaxpr/psum | solution.py:12
  1210.7 0.9 copy.35
  1211.7 0.9 fusion.67
  1212.5 11.7 cholesky.85
  1224.3 0.7 compare_reduce_fusion.2
  1225.6 9.8 custom-call.28
  1235.7 84.0 %all-reduce.4.cloned.1.call-done = f32[640,128]{1,0:T(8,128)} async-done(((f32[640,128]{1,0:T(8,128)}), f32[640,128]{1,0:T(8,128)}) %all-reduce.4.cloned.1.call-update) | async-done | bytes 327696 | tf_op jit(solution)/shard_map/while/body/eval_jaxpr/psum | solution.py:12
  1319.7 2.1 broadcast_select_fusion.4
  1322.5 97.5 %all-reduce.8.cloned.1.call-done = f32[5,128,128]{2,1,0:T(8,128)} async-done(((f32[5,128,128]{2,1,0:T(8,128)}), f32[5,128,128]{2,1,0:T(8,128)}) %all-reduce.8.cloned.1.call-update) | async-done | bytes 327696 | tf_op jit(solution)/shard_map/while/body/eval_jaxpr/psum | solution.py:12
  1420.0 1.1 broadcast_select_fusion.5
  1421.1 2.1 convolution_subtract_fusion.2
  1423.5 1.2 copy-done
  (61 shorter events, 8.1 us)
Async XLA Ops:
  9.8 4.0 copy-start.2
  9.8 31.8 %all-to-all-start = ((f32[2,3,2,128,384]{4,3,1,0,2:T(8,128)}), f32[2,3,2,128,384]{4,3,1,0,2:T(8,128)S(1)}, u32[]{:S(2)}, u32[]{:S(2)}) async-start(f32[2,3,2,128,384]{4,3,1,0,2:T(8,128)} %copy.23), calls=%async_computation | async-start | bytes 4718592 | tf_op jit(solution)/shard_map/all_to_all | solution.py:33
  50.8 6.3 copy-start.1
  57.8 243.7 %all-reduce.6.cloned.1.call-start = ((), (), s32[]{:S(2)}) async-start(), calls=%async_computation.2 | async-start | bytes 131072 | tf_op jit(solution)/shard_map/while/body/eval_jaxpr/psum | solution.py:12
  58.5 351.9 %all-reduce.4.cloned.1.call-start = ((), (), s32[]{:S(2)}) async-start(), calls=%async_computation.1 | async-start | bytes 655360 | tf_op jit(solution)/shard_map/while/body/eval_jaxpr/psum | solution.py:12
  59.4 451.4 %all-reduce.8.cloned.1.call-start = ((), (), s32[]{:S(2)}) async-start(), calls=%async_computation.3 | async-start | bytes 655360 | tf_op jit(solution)/shard_map/while/body/eval_jaxpr/psum | solution.py:12
  514.2 241.9 %all-reduce.6.cloned.1.call-start = ((), (), s32[]{:S(2)}) async-start(), calls=%async_computation.2 | async-start | bytes 131072 | tf_op jit(solution)/shard_map/while/body/eval_jaxpr/psum | solution.py:12
  515.0 349.9 %all-reduce.4.cloned.1.call-start = ((), (), s32[]{:S(2)}) async-start(), calls=%async_computation.1 | async-start | bytes 655360 | tf_op jit(solution)/shard_map/while/body/eval_jaxpr/psum | solution.py:12
  515.8 449.2 %all-reduce.8.cloned.1.call-start = ((), (), s32[]{:S(2)}) async-start(), calls=%async_computation.3 | async-start | bytes 655360 | tf_op jit(solution)/shard_map/while/body/eval_jaxpr/psum | solution.py:12
  968.5 242.2 %all-reduce.6.cloned.1.call-start = ((), (), s32[]{:S(2)}) async-start(), calls=%async_computation.2 | async-start | bytes 131072 | tf_op jit(solution)/shard_map/while/body/eval_jaxpr/psum | solution.py:12
  969.3 350.4 %all-reduce.4.cloned.1.call-start = ((), (), s32[]{:S(2)}) async-start(), calls=%async_computation.1 | async-start | bytes 655360 | tf_op jit(solution)/shard_map/while/body/eval_jaxpr/psum | solution.py:12
  970.1 449.9 %all-reduce.8.cloned.1.call-start = ((), (), s32[]{:S(2)}) async-start(), calls=%async_computation.3 | async-start | bytes 655360 | tf_op jit(solution)/shard_map/while/body/eval_jaxpr/psum | solution.py:12
  1423.5 1.2 copy-start
Sparse Core Ops, SparseCore 0:
  64.1 237.2 all-reduce.5
  303.8 106.6 all-reduce.3
  413.6 97.0 all-reduce.7
  520.2 235.8 all-reduce.5
  758.3 106.5 all-reduce.3
  867.9 97.0 all-reduce.7
  974.9 235.8 all-reduce.5
  1213.1 106.6 all-reduce.3
  1322.9 97.0 all-reduce.7
where the time goes:
time: 1430 us
  waiting for transfers between devices  1290 us (90%)
  other arithmetic  82.1 us (6%)
  matrix products  23.7 us (2%)
    psum x9, waiting for transfers between devices, from_root(): return lax.psum(kept, axis)  1270 us
    another operation x9, other arithmetic, eliminate(): factor = jnp.linalg.cholesky(diag_block)  37.3 us
    another operation x9, other arithmetic, eliminate(): inverse = jax.scipy.linalg.solve_triangular(factor, identity, lower=True)  33.3 us
  transfers between devices with their start and end apart: 10, of which 10 were waited for; matrix products, arithmetic and copies ran while one was open for 6% of the time, Pallas kernels for 0%

commit v1 on v0

v1 whole, which is shorter than its diff:
```python
import jax
import jax.numpy as jnp
from jax import lax
from jax.experimental import pallas as pl
from jax.experimental.pallas import tpu as pltpu
from jax.sharding import PartitionSpec as P

BS = 128
NPB = 3
LEAF = 8
F32 = jnp.float32
MESH = pl.DeviceIdType.MESH
HIGHEST = lax.Precision.HIGHEST
VMEM = pl.BlockSpec(memory_space=pltpu.VMEM)
SMEM = pl.BlockSpec(memory_space=pltpu.SMEM)
SOURCE = ((0, 0, 1), (2, 0, -1), (0, 1, 1))


def position():
    return lax.axis_index("sub"), lax.axis_index("row"), lax.axis_index("col")


def dot(a, b, dims):
    return lax.dot_general(a, b, (dims, ((), ())), precision=HIGHEST, preferred_element_type=F32)


def row_target(maps, child, local, row):
    return maps[child, local * 8 + row] // 16


def col_target(maps, child, m, col):
    return maps[child, m * 16 + col] // 16


def tile(ref, a, b):
    return ref.at[pl.ds(pl.multiple_of(a * BS, BS), BS), pl.ds(pl.multiple_of(b * BS, BS), BS)]


def prepare_kernel(maps, front, children, col_send, col_mine, row_send, row_mine, bulk):
    s, r, q = position()

    def block(c, local, m):
        return children[c, pl.ds(pl.multiple_of(local * BS, BS), BS), m * BS : (m + 1) * BS]

    @pl.when(q < NPB)
    def _():
        for n in range(5):
            col_mine[n] = front[n * BS : (n + 1) * BS, :BS]
            col_send[n] = jnp.zeros((BS, BS), F32)
        for c in range(2):
            for m in range(3):

                @pl.when(col_target(maps, 2 * s + c, m, q) == 0)
                def _():
                    for u in range(3):
                        a = row_target(maps, 2 * s + c, 2 * u + s, r)
                        col_mine[a] = col_mine[a] + block(c, 2 * u + s, m)
                        a = row_target(maps, 2 * s + c, 2 * u + 1 - s, r)
                        col_send[a] = col_send[a] + block(c, 2 * u + 1 - s, m)

    @pl.when(r < NPB)
    def _():
        for n in range(5):
            row_mine[n] = front[:BS, n * BS : (n + 1) * BS]
            row_send[n] = jnp.zeros((BS, BS), F32)
        for c in range(2):
            for u in range(3):

                @pl.when(row_target(maps, 2 * s + c, 2 * u, r) == 0)
                def _():
                    for m in range(3):
                        b = col_target(maps, 2 * s + c, m, q)

                        @pl.when(s == 0)
                        def _():
                            row_mine[b] = row_mine[b] + block(c, 2 * u, m)

                        @pl.when(s == 1)
                        def _():
                            row_send[b] = row_send[b] + block(c, 2 * u, m)

    for c in range(2):
        for u in range(3):
            bulk[c, u] = children[c, pl.ds(pl.multiple_of((2 * u + 1 - s) * BS, BS), BS), :]


def spread_kernel(col_send, col_mine, row_send, row_mine, left, right, corner,
                  col_recv, row_recv, xs, xr, zs, zr, ys, yr):
    s, r, q = position()
    x, y, z, core = 2 * lax.rem(r, 2) + s, r // 2, q // 2, lax.rem(q, 2)

    def at_x(d):
        nx = lax.rem(x + 4 + d, 4)
        return (lax.rem(nx, 2), 2 * y + nx // 2, q)

    def at_y(d):
        return (s, 2 * lax.rem(y + 4 + d, 4) + lax.rem(r, 2), q)

    def at_z(d):
        return (s, r, 2 * lax.rem(z + 8 + d, 8) + core)

    sibling = (s, r, 2 * z + 1 - core)
    partner = (1 - s, r, q)

    barrier = pltpu.get_barrier_semaphore()
    for peer in (at_x(1), at_x(-1), at_y(1), at_y(-1), at_z(1), at_z(-1), sibling):
        pl.semaphore_signal(barrier, inc=1, device_id=peer, device_id_type=MESH)
    pl.semaphore_wait(barrier, 7)

    def copy(src, dst, send, recv, device):
        return pltpu.make_async_remote_copy(
            src_ref=src, dst_ref=dst, send_sem=send, recv_sem=recv, device_id=device, device_id_type=MESH
        )

    def col_copy(n):
        return copy(col_send.at[n], col_recv.at[n], xs.at[0, n], xr.at[0, n], partner)

    def row_copy(n):
        return copy(row_send.at[n], row_recv.at[n], xs.at[1, n], xr.at[1, n], partner)

    col_on = q < NPB
    row_out = (r < NPB) & (s == 1)

    def exchange(act):
        @pl.loop(0, 5)
        def _(n):
            @pl.when(col_on)
            def _():
                act(col_copy(n))

            @pl.when(row_out)
            def _():
                act(row_copy(n))

    exchange(lambda c: c.start())

    def line_sends(k, n, act):
        zk, ck = k // 2, k % 2
        dz = lax.rem(z - zk + 8, 8)
        on = core == ck
        here = left.at[k, n]

        @pl.when(on & (dz <= 3))
        def _():
            act(copy(here, here, zs.at[k, n, 0], zr.at[k, n], at_z(1)))

        @pl.when(on & ((dz == 0) | (dz >= 6)))
        def _():
            act(copy(here, here, zs.at[k, n, 1], zr.at[k, n], at_z(-1)))

        @pl.when(on)
        def _():
            act(copy(here, here, zs.at[k, n, 2], zr.at[k, n], sibling))

    def line_step(k, n):
        @pl.when(q == k)
        def _():
            col_copy(n).wait_recv()
            left[k, n] = col_mine[n] + col_recv[n]

        @pl.when(q != k)
        def _():
            copy(left.at[k, n], left.at[k, n], zs.at[k, n, 0], zr.at[k, n], sibling).wait_recv()

        line_sends(k, n, lambda c: c.start())

    def offsets(i):
        xi, yi, g = SOURCE[i]
        return lax.rem(g * (x - xi) + 4, 4), lax.rem(y - yi + 4, 4), g

    def plane_sends(i, here, slot, act):
        dx, dy, g = offsets(i)
        along_x = (core == 1) | (dy == 0)
        along_y = (core == 0) | (dx == 0)

        @pl.when(along_x & (dx <= 1))
        def _():
            act(copy(here, here, ys.at[i, slot, 0], yr.at[i, slot], at_x(g)))

        @pl.when(along_x & (dx == 0))
        def _():
            act(copy(here, here, ys.at[i, slot, 1], yr.at[i, slot], at_x(-g)))

        @pl.when(along_y & (dy <= 1))
        def _():
            act(copy(here, here, ys.at[i, slot, 2], yr.at[i, slot], at_y(1)))

        @pl.when(along_y & (dy == 0))
        def _():
            act(copy(here, here, ys.at[i, slot, 3], yr.at[i, slot], at_y(-1)))

    def plane_step(i, here, slot, make):
        dx, dy, _ = offsets(i)
        source = (dx == 0) & (dy == 0)
        pl.when(source)(make)

        @pl.when(jnp.logical_not(source))
        def _():
            copy(here, here, ys.at[i, slot, 0], yr.at[i, slot], sibling).wait_recv()

        plane_sends(i, here, slot, lambda c: c.start())

    def row_make(i, n):
        def make():
            row_copy(n).wait_recv()
            right[i, n] = row_mine[n] + row_recv[n]

        return make

    def corner_make(i, k):
        def make():
            corner[i, k] = left[k, 0]

        return make

    corners = [(i, k) for i in range(NPB) for k in range(i + 1)]
    for k in range(NPB):
        line_step(k, 0)
    for i, k in corners:
        plane_step(i, corner.at[i, k], 5 + k, corner_make(i, k))
    for i in range(NPB):
        plane_step(i, right.at[i, 0], 0, row_make(i, 0))

    @pl.loop(1, 5)
    def _(n):
        for k in range(NPB):
            line_step(k, n)
        for i in range(NPB):
            plane_step(i, right.at[i, n], n, row_make(i, n))

    exchange(lambda c: c.wait_send())
    for i, k in corners:
        plane_sends(i, corner.at[i, k], 5 + k, lambda c: c.wait_send())

    @pl.loop(0, 5)
    def _(n):
        for k in range(NPB):
            line_sends(k, n, lambda c: c.wait_send())
        for i in range(NPB):
            plane_sends(i, right.at[i, n], n, lambda c: c.wait_send())


def lanes(v, j):
    return jnp.take_along_axis(v, jnp.full((8, BS), j, jnp.int32), axis=1)


def sublanes(v, i):
    return jnp.broadcast_to(v[i : i + 1, :], (8, BS))


def factor_block(block):
    row = lax.broadcasted_iota(jnp.int32, (8, BS), 0)
    lane = lax.broadcasted_iota(jnp.int32, (8, BS), 1)
    tiles = BS // LEAF
    wa = [block[8 * t : 8 * t + 8] for t in range(tiles)]
    wi = [jnp.where(lane == row + 8 * t, 1.0, 0.0).astype(F32) for t in range(tiles)]
    upper, inverse = [], []
    for t in range(tiles):
        cols = {w: [lanes(wa[w], 8 * t + m) for m in range(8)] for w in range(t, tiles)}
        sc = [[sublanes(cols[t][n], m) if n <= m else None for n in range(8)] for m in range(8)]
        low = [[None] * 8 for _ in range(8)]
        rs, ua, ui = [None] * 8, [None] * 8, [None] * 8
        for m in range(8):
            rs[m] = lax.rsqrt(sc[m][m])
            for i in range(m + 1, 8):
                low[i][m] = sc[i][m] * rs[m]
            for i in range(m + 1, 8):
                for j in range(m + 1, i + 1):
                    sc[i][j] = sc[i][j] - low[i][m] * low[j][m]
            ga, gi = sublanes(wa[t], m), sublanes(wi[t], m)
            for n in range(m):
                ga = ga - low[m][n] * ua[n]
                gi = gi - low[m][n] * ui[n]
            ua[m], ui[m] = ga * rs[m], gi * rs[m]
        up, inv = ua[0], ui[0]
        for m in range(1, 8):
            up = jnp.where(row == m, ua[m], up)
            inv = jnp.where(row == m, ui[m], inv)
        upper.append(jnp.where(lane >= row + 8 * t, up, 0.0))
        inverse.append(jnp.where(lane <= row + 8 * t, inv, 0.0))
        if t == tiles - 1:
            break
        ya, yi = [None] * 8, [None] * 8
        for m in reversed(range(8)):
            a, b = ua[m], ui[m]
            for n in range(m + 1, 8):
                a = a - low[n][m] * ya[n]
                b = b - low[n][m] * yi[n]
            ya[m], yi[m] = a * rs[m], b * rs[m]
        for w in range(t + 1, tiles):
            a, b = wa[w], wi[w]
            for m in range(8):
                a = a - cols[w][m] * ya[m]
                b = b - cols[w][m] * yi[m]
            wa[w], wi[w] = a, b
    return jnp.concatenate(upper, 0), jnp.concatenate(inverse, 0)


ROWS_T = ((1,), (1,))
PLAIN = ((1,), (0,))


def place(maps, base, c, s, r, q, local, read):
    for u in range(3):
        a = row_target(maps, c, local(u), r)
        for m in range(3):
            b = col_target(maps, c, m, q)
            t = tile(base, a, b)
            t[...] = t[...] + read(u, m)


def factor_kernel(maps, corner, left, right, front, children, panel, upper, base, pr):
    s, r, q = position()
    d = {(i, k): corner[i, k] for i in range(NPB) for k in range(i + 1)}
    for k in range(NPB):
        up, inv = factor_block(d[k, k])
        upper[k] = up
        low = {}
        for i in range(k + 1, NPB):
            low[i] = dot(d[i, k], inv, ROWS_T)
        for i in range(k + 1, NPB):
            for j in range(k + 1, i + 1):
                d[i, j] = d[i, j] - dot(low[i], low[j], ROWS_T)
        mine = left[k].reshape(5 * BS, BS)
        for i in range(k):
            mine = mine - dot(panel[:, i * BS : (i + 1) * BS], lows[k, i], ROWS_T)
        panel[:, k * BS : (k + 1) * BS] = dot(mine, inv, ROWS_T)
        for n in range(5):
            other = right[k, n]
            for i in range(k):
                other = other - dot(lows[k, i], pr[i * BS : (i + 1) * BS, n * BS : (n + 1) * BS], PLAIN)
            pr[k * BS : (k + 1) * BS, n * BS : (n + 1) * BS] = dot(inv, other, PLAIN)
        if k == 0:
            lows = {}
        for i in low:
            lows[i, k] = low[i]

    for a in range(5):
        rows = slice(a * BS, (a + 1) * BS)
        base[rows, :] = front[rows, :] - dot(panel[rows, :], pr[...], PLAIN)
    for c in range(2):
        place(
            maps, base, 2 * s + c, s, r, q, lambda u: 2 * u + s,
            lambda u, m: children[c, pl.ds(pl.multiple_of((2 * u + s) * BS, BS), BS), m * BS : (m + 1) * BS],
        )


def finish_kernel(maps, base, arrived, panel, upper, out):
    s, r, q = position()
    dev_row = 8 * s + r
    out[...] = base[...]
    for c in range(2):
        place(
            maps, out, 2 * (1 - s) + c, s, r, q, lambda u: 2 * u + s,
            lambda u, m: arrived[c, u, :, m * BS : (m + 1) * BS],
        )

    @pl.when(q < NPB)
    def _():
        lane = pl.ds(pl.multiple_of(q * BS, BS), BS)
        out[BS:, :BS] = panel[BS:, lane]

        @pl.when(dev_row > q)
        def _():
            out[:BS, :BS] = panel[:BS, lane]

        @pl.when(dev_row == q)
        def _():
            out[:BS, :BS] = upper[q].T

    @pl.when(dev_row < NPB)
    def _():
        out[:BS, BS:] = jnp.zeros((BS, 4 * BS), F32)

        @pl.when(q > dev_row)
        def _():
            out[:BS, :BS] = jnp.zeros((BS, BS), F32)


def shape(*dims):
    return jax.ShapeDtypeStruct(dims, F32)


def body(front, children, child_maps):
    col_send, col_mine, row_send, row_mine, bulk = pl.pallas_call(
        prepare_kernel,
        out_shape=[shape(5, BS, BS)] * 4 + [shape(2, 3, BS, 3 * BS)],
        in_specs=[SMEM, VMEM, VMEM],
        out_specs=[VMEM] * 5,
        name="prepare",
    )(child_maps, front, children)
    dma = pltpu.SemaphoreType.DMA
    left, right, corner = pl.pallas_call(
        spread_kernel,
        out_shape=[shape(NPB, 5, BS, BS), shape(NPB, 5, BS, BS), shape(NPB, NPB, BS, BS)],
        in_specs=[VMEM] * 4,
        out_specs=[VMEM] * 3,
        scratch_shapes=[
            pltpu.VMEM((5, BS, BS), F32),
            pltpu.VMEM((5, BS, BS), F32),
            dma((2, 5)),
            dma((2, 5)),
            dma((NPB, 5, 3)),
            dma((NPB, 5)),
            dma((NPB, 8, 4)),
            dma((NPB, 8)),
        ],
        compiler_params=pltpu.CompilerParams(collective_id=0, has_side_effects=True),
        name="spread",
    )(col_send, col_mine, row_send, row_mine)
    bulk, corner = lax.optimization_barrier((bulk, corner))
    arrived = lax.ppermute(bulk, "sub", [(0, 1), (1, 0)])
    panel, upper, base = pl.pallas_call(
        factor_kernel,
        out_shape=[shape(5 * BS, NPB * BS), shape(NPB, BS, BS), shape(5 * BS, 5 * BS)],
        in_specs=[SMEM] + [VMEM] * 5,
        out_specs=[VMEM] * 3,
        scratch_shapes=[pltpu.VMEM((NPB * BS, 5 * BS), F32)],
        cost_estimate=pl.CostEstimate(flops=10**10, bytes_accessed=10**8, transcendentals=0),
        name="factor",
    )(child_maps, corner, left, right, front, children)
    return pl.pallas_call(
        finish_kernel,
        out_shape=shape(5 * BS, 5 * BS),
        in_specs=[SMEM] + [VMEM] * 4,
        out_specs=VMEM,
        name="finish",
    )(child_maps, base, arrived, panel, upper)


def solution(mesh):
    return jax.shard_map(
        body,
        mesh=mesh,
        in_specs=(P(("sub", "row"), "col"), P("sub", "row", "col"), P()),
        out_specs=P(("sub", "row"), "col"),
        check_vma=False,
    )
```

time: 1430 us -> 231 us (0.16)
  waiting for transfers between devices: 1290 us -> 0.49 us
  Pallas kernels: 0 us -> 222 us
  other arithmetic: 82.1 us -> 0 us
  matrix products: 23.7 us -> 0 us
    psum x9 -> x0, waiting for transfers between devices: 1270 us -> none  [from_root(): return lax.psum(kept, axis)]
    pallas_call x0 -> x4, Pallas kernels: none -> 222 us  [the longest x1 190 us: body(): pl.pallas_call(spread_kernel, out_shape=[shape(NPB, 5, BS, BS), shape(NPB...]
    another operation x18 -> x0, other arithmetic: 70.5 us -> none  [the longest x9 37.3 us: eliminate(): factor = jnp.linalg.cholesky(diag_block)]
    all_to_all x1 -> x0, waiting for transfers between devices: 26.5 us -> none  [body(): lax.all_to_all(pieces, 'sub', split_axis=2, concat_axis=0, tiled=True)]
    dot_general x8 -> x0, matrix products: 22.9 us -> none  [the longest x3 6.39 us: eliminate(): panel_rows = jnp.dot(column_in, inverse.T, precision=highest)]
  transfers between devices with their start and end apart: 10 -> 1, of which waited for: 10 -> 1; matrix products, arithmetic and copies ran while one was open for 6% -> 0% of each run, Pallas kernels for 0% -> 10%
where the time goes in v1:
time: 231 us; the launch traced here: 228 us
  Pallas kernels  222 us (96%)
  starting transfers between devices  4.56 us (2%)
    pallas_call x1, Pallas kernels, body(): pl.pallas_call(spread_kernel, out_shape=[shape(NPB, 5, BS, BS), shape(NPB...  190 us
    pallas_call x1, Pallas kernels, body(): pl.pallas_call(factor_kernel, out_shape=[shape(5 * BS, NPB * BS), shape(N...  23.8 us
  transfers between devices with their start and end apart: 1, of which 1 were waited for; matrix products, arithmetic and copies ran while one was open for 0% of the time, Pallas kernels for 10%

profile of v1, /device:TPU:160, one launch (start us, length us, event | category | flops | bytes accessed | tf_op | source)
XLA Modules:
  0.0 227.7 jit_solution(18010029642671393911)
XLA Ops:
  0.0 3.9 %prepare.1 = (f32[5,128,128]{2,1,0:T(8,128)}, f32[5,128,128]{2,1,0:T(8,128)}, f32[5,128,128]{2,1,0:T(8,128)}, f32[5,128,128]{2,1,0:T(8,128)}, f32[2,3,128,384]{3,2,1,0:T(8,128)}) custom-call(s32[4,48]{1,0:T(4,128)} %maps.5, f32[640,640]{1,0:T(8,128)} %front.3, f32[2,768,384]{2,1,0:T(8,128)} %children.3), custom_call_target="tpu_custom_call" | custom-call | tf_op jit(solution)/shard_map/prepare/pallas_call | solution.py:385
  3.9 190.4 %spread.1 = (f32[3,5,128,128]{3,2,1,0:T(8,128)}, f32[3,5,128,128]{3,2,1,0:T(8,128)}, f32[3,3,128,128]{3,2,1,0:T(8,128)}) custom-call(f32[5,128,128]{2,1,0:T(8,128)} %get-tuple-element.19.col_send, f32[5,128,128]{2,1,0:T(8,128)} %get-tuple-element.20.col_mine, f32[5,128,128]{2,1,0:T(8,128)} %get-tuple-element.21.row_send, ...), custom_call_target="tpu_custom_call" | custom-call | tf_op jit(solution)/shard_map/spread/pallas_call | solution.py:393
  194.3 4.6 %collective-permute-start = (f32[2,3,128,384]{3,2,1,0:T(8,128)}, f32[2,3,128,384]{3,2,1,0:T(8,128)S(1)}, u32[]{:S(2)}, u32[]{:S(2)}) collective-permute-start(f32[2,3,128,384]{3,2,1,0:T(8,128)} %get-tuple-element.28), channel_id=1, source_target_pairs={{0,128},{128,0},{1,129},{129,1},{2,130},{130,2},{3,131},{131,3},{4... | collective-permute-start | bytes 3538952 | tf_op jit(solution)/shard_map/ppermute | solution.py:412
  198.8 23.8 %factor.1 = (f32[640,384]{1,0:T(8,128)}, f32[3,128,128]{2,1,0:T(8,128)}, f32[640,640]{1,0:T(8,128)}) custom-call(s32[4,48]{1,0:T(4,128)} %maps.5, f32[3,3,128,128]{3,2,1,0:T(8,128)} %get-tuple-element.24.corner, f32[3,5,128,128]{3,2,1,0:T(8,128)} %get-tuple-element.25.left, f32[3,5,128,128]{3,2,1,0:T(8,128)} %get-tuple-element.26.right, f32[640,640]{1,0:T(8,128)} %front.3, ...), custom_call_target="tpu_custom_call" | custom-call | flops 10000000000 | bytes 100000000 | tf_op jit(solution)/shard_map/factor/pallas_call | solution.py:413
  222.6 0.5 collective-permute-done.arrived
  223.1 0.0 copy-start
  223.1 1.0 copy-done
  224.2 3.5 %finish.1 = f32[640,640]{1,0:T(8,128)} custom-call(s32[4,48]{1,0:T(4,128)} %maps.5, f32[640,640]{1,0:T(8,128)} %get-tuple-element.27.base, f32[2,3,128,384]{3,2,1,0:T(8,128)} %copy-done, f32[640,384]{1,0:T(8,128)} %get-tuple-element.29.panel, f32[3,128,128]{2,1,0:T(8,128)} %get-tuple-element.30.upper), custom_call_target="tpu_custom_call" | custom-call | tf_op jit(solution)/shard_map/finish/pallas_call | solution.py:422
Async XLA Ops:
  194.3 28.8 %collective-permute-start = (f32[2,3,128,384]{3,2,1,0:T(8,128)}, f32[2,3,128,384]{3,2,1,0:T(8,128)S(1)}, u32[]{:S(2)}, u32[]{:S(2)}) collective-permute-start(f32[2,3,128,384]{3,2,1,0:T(8,128)} %get-tuple-element.28), channel_id=1, source_target_pairs={{0,128},{128,0},{1,129},{129,1},{2,130},{130,2},{3,131},{131,3},{4... | collective-permute-start | bytes 3538952 | tf_op jit(solution)/shard_map/ppermute | solution.py:412
  223.1 1.0 copy-start

commit v2 on v1

--- a/solution.py
+++ b/solution.py
@@ -134,10 +134,15 @@
 
     exchange(lambda c: c.start())
 
-    def line_sends(k, n, act):
+    def line_place(k):
         zk, ck = k // 2, k % 2
         dz = lax.rem(z - zk + 8, 8)
         on = core == ck
+        hops = jnp.where(dz <= 4, dz, 8 - dz) + jnp.where(on, 0, 1)
+        return dz, on, hops
+
+    def line_sends(k, n, act):
+        dz, on, _ = line_place(k)
         here = left.at[k, n]
 
         @pl.when(on & (dz <= 3))
@@ -164,12 +169,14 @@
 
         line_sends(k, n, lambda c: c.start())
 
-    def offsets(i):
+    def plane_place(i):
         xi, yi, g = SOURCE[i]
-        return lax.rem(g * (x - xi) + 4, 4), lax.rem(y - yi + 4, 4), g
+        dx, dy = lax.rem(g * (x - xi) + 4, 4), lax.rem(g * (y - yi) + 4, 4)
+        hops = jnp.where(dx == 3, 1, dx) + jnp.where(dy == 3, 1, dy)
+        return dx, dy, g, hops
 
     def plane_sends(i, here, slot, act):
-        dx, dy, g = offsets(i)
+        dx, dy, g, _ = plane_place(i)
         along_x = (core == 1) | (dy == 0)
         along_y = (core == 0) | (dx == 0)
 
@@ -183,18 +190,17 @@
 
         @pl.when(along_y & (dy <= 1))
         def _():
-            act(copy(here, here, ys.at[i, slot, 2], yr.at[i, slot], at_y(1)))
+            act(copy(here, here, ys.at[i, slot, 2], yr.at[i, slot], at_y(g)))
 
         @pl.when(along_y & (dy == 0))
         def _():
-            act(copy(here, here, ys.at[i, slot, 3], yr.at[i, slot], at_y(-1)))
+            act(copy(here, here, ys.at[i, slot, 3], yr.at[i, slot], at_y(-g)))
 
     def plane_step(i, here, slot, make):
-        dx, dy, _ = offsets(i)
-        source = (dx == 0) & (dy == 0)
-        pl.when(source)(make)
-
-        @pl.when(jnp.logical_not(source))
+        _, _, _, hops = plane_place(i)
+        pl.when(hops == 0)(make)
+
+        @pl.when(hops > 0)
         def _():
             copy(here, here, ys.at[i, slot, 0], yr.at[i, slot], sibling).wait_recv()
 
@@ -214,19 +220,28 @@
         return make
 
     corners = [(i, k) for i in range(NPB) for k in range(i + 1)]
-    for k in range(NPB):
-        line_step(k, 0)
-    for i, k in corners:
-        plane_step(i, corner.at[i, k], 5 + k, corner_make(i, k))
-    for i in range(NPB):
-        plane_step(i, right.at[i, 0], 0, row_make(i, 0))
-
-    @pl.loop(1, 5)
-    def _(n):
+
+    @pl.loop(0, 10)
+    def _(slot):
         for k in range(NPB):
-            line_step(k, n)
+            n = slot - line_place(k)[2]
+
+            @pl.when((n >= 0) & (n < 5))
+            def _():
+                line_step(k, n)
+
+        for i, k in corners:
+
+            @pl.when(slot == line_place(k)[2] + plane_place(i)[3])
+            def _():
+                plane_step(i, corner.at[i, k], 5 + k, corner_make(i, k))
+
         for i in range(NPB):
-            plane_step(i, right.at[i, n], n, row_make(i, n))
+            n = slot - plane_place(i)[3]
+
+            @pl.when((n >= 0) & (n < 5))
+            def _():
+                plane_step(i, right.at[i, n], n, row_make(i, n))
 
     exchange(lambda c: c.wait_send())
     for i, k in corners:

time: 231 us -> 83.2 us (0.36); the launches traced: 228 us -> 83.1 us
  Pallas kernels: 222 us -> 76.9 us
  waiting for transfers between devices: 0.49 us -> 4.83 us
  starting transfers between devices: 4.56 us -> 0.27 us
    pallas_call x1, Pallas kernels: 190 us -> 45.6 us  [body(): pl.pallas_call(spread_kernel, out_shape=[shape(NPB, 5, BS, BS), shape(NPB...]
    ppermute x1, waiting for transfers between devices: 0.49 us -> 4.83 us  [body(): arrived = lax.ppermute(bulk, 'sub', [(0, 1), (1, 0)])]
    ppermute x1, starting transfers between devices: 4.56 us -> 0.27 us  [body(): arrived = lax.ppermute(bulk, 'sub', [(0, 1), (1, 0)])]
  transfers between devices with their start and end apart: 1 -> 1, of which waited for: 1 -> 1; matrix products, arithmetic and copies ran while one was open for 0% -> 0% of each run, Pallas kernels for 10% -> 29%
where the time goes in v2:
time: 83.2 us; the launch traced here: 83.1 us
  Pallas kernels  76.9 us (92%)
  waiting for transfers between devices  4.83 us (6%)
  local copies, waits for them, and re-layouts  1.04 us (1%)
    pallas_call x1, Pallas kernels, body(): pl.pallas_call(spread_kernel, out_shape=[shape(NPB, 5, BS, BS), shape(NPB...  45.6 us
    pallas_call x1, Pallas kernels, body(): pl.pallas_call(factor_kernel, out_shape=[shape(5 * BS, NPB * BS), shape(N...  23.8 us
    ppermute x1, waiting for transfers between devices, body(): arrived = lax.ppermute(bulk, 'sub', [(0, 1), (1, 0)])  4.83 us
    pallas_call x1, Pallas kernels, body(): pl.pallas_call(prepare_kernel, out_shape=[shape(5, BS, BS)] * 4 + [shape(...  3.96 us
    pallas_call x1, Pallas kernels, body(): pl.pallas_call(finish_kernel, out_shape=shape(5 * BS, 5 * BS), in_specs=[...  3.54 us
  transfers between devices with their start and end apart: 1, of which 1 were waited for; matrix products, arithmetic and copies ran while one was open for 0% of the time, Pallas kernels for 29%

profile of v2, /device:TPU:160, one launch (start us, length us, event | category | flops | bytes accessed | tf_op | source)
XLA Modules:
  0.0 83.1 jit_solution(14857214196686417395)
XLA Ops:
  0.0 4.0 %prepare.1 = (f32[5,128,128]{2,1,0:T(8,128)}, f32[5,128,128]{2,1,0:T(8,128)}, f32[5,128,128]{2,1,0:T(8,128)}, f32[5,128,128]{2,1,0:T(8,128)}, f32[2,3,128,384]{3,2,1,0:T(8,128)}) custom-call(s32[4,48]{1,0:T(4,128)} %maps.5, f32[640,640]{1,0:T(8,128)} %front.3, f32[2,768,384]{2,1,0:T(8,128)} %children.3), custom_call_target="tpu_custom_call" | custom-call | tf_op jit(solution)/shard_map/prepare/pallas_call | solution.py:400
  4.0 45.6 %spread.1 = (f32[3,5,128,128]{3,2,1,0:T(8,128)}, f32[3,5,128,128]{3,2,1,0:T(8,128)}, f32[3,3,128,128]{3,2,1,0:T(8,128)}) custom-call(f32[5,128,128]{2,1,0:T(8,128)} %get-tuple-element.19.col_send, f32[5,128,128]{2,1,0:T(8,128)} %get-tuple-element.20.col_mine, f32[5,128,128]{2,1,0:T(8,128)} %get-tuple-element.21.row_send, ...), custom_call_target="tpu_custom_call" | custom-call | tf_op jit(solution)/shard_map/spread/pallas_call | solution.py:408
  49.6 0.3 collective-permute-start
  49.9 23.8 %factor.1 = (f32[640,384]{1,0:T(8,128)}, f32[3,128,128]{2,1,0:T(8,128)}, f32[640,640]{1,0:T(8,128)}) custom-call(s32[4,48]{1,0:T(4,128)} %maps.5, f32[3,3,128,128]{3,2,1,0:T(8,128)} %get-tuple-element.24.corner, f32[3,5,128,128]{3,2,1,0:T(8,128)} %get-tuple-element.25.left, f32[3,5,128,128]{3,2,1,0:T(8,128)} %get-tuple-element.26.right, f32[640,640]{1,0:T(8,128)} %front.3, ...), custom_call_target="tpu_custom_call" | custom-call | flops 10000000000 | bytes 100000000 | tf_op jit(solution)/shard_map/factor/pallas_call | solution.py:428
  73.7 4.8 %collective-permute-done.arrived = f32[2,3,128,384]{3,2,1,0:T(8,128)S(1)} collective-permute-done((f32[2,3,128,384]{3,2,1,0:T(8,128)}, f32[2,3,128,384]{3,2,1,0:T(8,128)S(1)}, u32[]{:S(2)}, u32[]{:S(2)}) %collective-permute-start) | collective-permute-done | bytes 1179680 | tf_op jit(solution)/shard_map/ppermute | solution.py:427
  78.5 0.0 copy-start
  78.5 1.0 %copy-done = f32[2,3,128,384]{3,2,1,0:T(8,128)} copy-done((f32[2,3,128,384]{3,2,1,0:T(8,128)}, f32[2,3,128,384]{3,2,1,0:T(8,128)S(1)}, u32[]{:S(2)}) %copy-start) | copy-done | bytes 1179672
  79.5 3.5 %finish.1 = f32[640,640]{1,0:T(8,128)} custom-call(s32[4,48]{1,0:T(4,128)} %maps.5, f32[640,640]{1,0:T(8,128)} %get-tuple-element.27.base, f32[2,3,128,384]{3,2,1,0:T(8,128)} %copy-done, f32[640,384]{1,0:T(8,128)} %get-tuple-element.29.panel, f32[3,128,128]{2,1,0:T(8,128)} %get-tuple-element.30.upper), custom_call_target="tpu_custom_call" | custom-call | tf_op jit(solution)/shard_map/finish/pallas_call | solution.py:437
Async XLA Ops:
  49.6 28.9 %collective-permute-start = (f32[2,3,128,384]{3,2,1,0:T(8,128)}, f32[2,3,128,384]{3,2,1,0:T(8,128)S(1)}, u32[]{:S(2)}, u32[]{:S(2)}) collective-permute-start(f32[2,3,128,384]{3,2,1,0:T(8,128)} %get-tuple-element.28), channel_id=1, source_target_pairs={{0,128},{128,0},{1,129},{129,1},{2,130},{130,2},{3,131},{131,3},{4... | collective-permute-start | bytes 3538952 | tf_op jit(solution)/shard_map/ppermute | solution.py:427
  78.5 1.0 %copy-start = (f32[2,3,128,384]{3,2,1,0:T(8,128)}, f32[2,3,128,384]{3,2,1,0:T(8,128)S(1)}, u32[]{:S(2)}) copy-start(f32[2,3,128,384]{3,2,1,0:T(8,128)S(1)} %collective-permute-done.arrived) | copy-start | bytes 3538948

commit v3 on v2

--- a/solution.py
+++ b/solution.py
@@ -13,6 +13,7 @@
 HIGHEST = lax.Precision.HIGHEST
 VMEM = pl.BlockSpec(memory_space=pltpu.VMEM)
 SMEM = pl.BlockSpec(memory_space=pltpu.SMEM)
+ANY = pl.BlockSpec(memory_space=pl.ANY)
 SOURCE = ((0, 0, 1), (2, 0, -1), (0, 1, 1))
 
 
@@ -36,7 +37,7 @@
     return ref.at[pl.ds(pl.multiple_of(a * BS, BS), BS), pl.ds(pl.multiple_of(b * BS, BS), BS)]
 
 
-def prepare_kernel(maps, front, children, col_send, col_mine, row_send, row_mine, bulk):
+def prepare_kernel(maps, front, children, col_send, col_mine, row_send, row_mine, bulk, base):
     s, r, q = position()
 
     def block(c, local, m):
@@ -82,10 +83,18 @@
     for c in range(2):
         for u in range(3):
             bulk[c, u] = children[c, pl.ds(pl.multiple_of((2 * u + 1 - s) * BS, BS), BS), :]
-
-
-def spread_kernel(col_send, col_mine, row_send, row_mine, left, right, corner,
-                  col_recv, row_recv, xs, xr, zs, zr, ys, yr):
+    base[...] = front[...]
+    for c in range(2):
+        for u in range(3):
+            a = row_target(maps, 2 * s + c, 2 * u + s, r)
+            for m in range(3):
+                t = tile(base, a, col_target(maps, 2 * s + c, m, q))
+                t[...] = t[...] + block(c, 2 * u + s, m)
+
+
+def eliminate_kernel(col_send, col_mine, row_send, row_mine, bulk, assembled, base, arrived,
+                     left, right, corner, work, lows, inverses, uppers, panel, pr,
+                     col_recv, row_recv, xs, xr, zs, zr, ys, yr, bs, br):
     s, r, q = position()
     x, y, z, core = 2 * lax.rem(r, 2) + s, r // 2, q // 2, lax.rem(q, 2)
 
@@ -120,6 +129,11 @@
 
     col_on = q < NPB
     row_out = (r < NPB) & (s == 1)
+
+    def bulk_copies(act):
+        for c in range(2):
+            for u in range(3):
+                act(copy(bulk.at[c, u], arrived.at[c, u], bs.at[c, u], br.at[c, u], partner))
 
     def exchange(act):
         @pl.loop(0, 5)
@@ -177,8 +191,7 @@
 
     def plane_sends(i, here, slot, act):
         dx, dy, g, _ = plane_place(i)
-        along_x = (core == 1) | (dy == 0)
-        along_y = (core == 0) | (dx == 0)
+        along_x = dy == 0
 
         @pl.when(along_x & (dx <= 1))
         def _():
@@ -188,11 +201,11 @@
         def _():
             act(copy(here, here, ys.at[i, slot, 1], yr.at[i, slot], at_x(-g)))
 
-        @pl.when(along_y & (dy <= 1))
+        @pl.when(dy <= 1)
         def _():
             act(copy(here, here, ys.at[i, slot, 2], yr.at[i, slot], at_y(g)))
 
-        @pl.when(along_y & (dy == 0))
+        @pl.when(dy == 0)
         def _():
             act(copy(here, here, ys.at[i, slot, 3], yr.at[i, slot], at_y(-g)))
 
@@ -224,17 +237,28 @@
     @pl.loop(0, 10)
     def _(slot):
         for k in range(NPB):
-            n = slot - line_place(k)[2]
-
-            @pl.when((n >= 0) & (n < 5))
+
+            @pl.when(slot == line_place(k)[2])
+            def _():
+                line_step(k, 0)
+
+        for i, k in corners:
+
+            @pl.when(slot == line_place(k)[2] + plane_place(i)[3])
+            def _():
+                plane_step(i, corner.at[i, k], 5 + k, corner_make(i, k))
+
+    bulk_copies(lambda c: c.start())
+    for i, k in corners:
+        work[i, k] = corner[i, k]
+
+    def rest(slot):
+        for k in range(NPB):
+            n = slot - line_place(k)[2] + 1
+
+            @pl.when((n >= 1) & (n < 5))
             def _():
                 line_step(k, n)
-
-        for i, k in corners:
-
-            @pl.when(slot == line_place(k)[2] + plane_place(i)[3])
-            def _():
-                plane_step(i, corner.at[i, k], 5 + k, corner_make(i, k))
 
         for i in range(NPB):
             n = slot - plane_place(i)[3]
@@ -243,6 +267,67 @@
             def _():
                 plane_step(i, right.at[i, n], n, row_make(i, n))
 
+    @pl.loop(0, NPB)
+    def _(k):
+        def after(t):
+            if t % 5 == 4:
+                rest(3 * k + t // 5)
+
+        factor_block(work.at[k, k], uppers.at[k], inverses.at[k], after)
+        inv = inverses[k]
+        for i in range(1, NPB):
+
+            @pl.when(i > k)
+            def _():
+                lows[i, k] = dot(work[i, k], inv, ROWS_T)
+
+        for i in range(1, NPB):
+            for j in range(1, i + 1):
+
+                @pl.when(j > k)
+                def _():
+                    work[i, j] = work[i, j] - dot(lows[i, k], lows[j, k], ROWS_T)
+
+    for k in range(NPB):
+        inv = inverses[k]
+        mine = left[k].reshape(5 * BS, BS)
+        for i in range(k):
+            mine = mine - dot(panel[:, i * BS : (i + 1) * BS], lows[k, i], ROWS_T)
+        panel[:, k * BS : (k + 1) * BS] = dot(mine, inv, ROWS_T)
+        for n in range(5):
+            other = right[k, n]
+            for i in range(k):
+                other = other - dot(lows[k, i], pr[i * BS : (i + 1) * BS, n * BS : (n + 1) * BS], PLAIN)
+            pr[k * BS : (k + 1) * BS, n * BS : (n + 1) * BS] = dot(inv, other, PLAIN)
+
+    for a in range(5):
+        rows = slice(a * BS, (a + 1) * BS)
+        base[rows, :] = assembled[rows, :] - dot(panel[rows, :], pr[...], PLAIN)
+
+    dev_row = 8 * s + r
+    for k in range(NPB):
+
+        @pl.when(q == k)
+        def _():
+            base[BS:, :BS] = panel[BS:, k * BS : (k + 1) * BS]
+
+            @pl.when(dev_row > k)
+            def _():
+                base[:BS, :BS] = panel[:BS, k * BS : (k + 1) * BS]
+
+            @pl.when(dev_row == k)
+            def _():
+                base[:BS, :BS] = uppers[k].T
+
+    @pl.when(dev_row < NPB)
+    def _():
+        base[:BS, BS:] = jnp.zeros((BS, 4 * BS), F32)
+
+        @pl.when(q > dev_row)
+        def _():
+            base[:BS, :BS] = jnp.zeros((BS, BS), F32)
+
+    bulk_copies(lambda c: c.wait())
     exchange(lambda c: c.wait_send())
     for i, k in corners:
         plane_sends(i, corner.at[i, k], 5 + k, lambda c: c.wait_send())
@@ -263,13 +348,12 @@
     return jnp.broadcast_to(v[i : i + 1, :], (8, BS))
 
 
-def factor_block(block):
+def factor_block(block, upper, inverse, after):
     row = lax.broadcasted_iota(jnp.int32, (8, BS), 0)
     lane = lax.broadcasted_iota(jnp.int32, (8, BS), 1)
     tiles = BS // LEAF
-    wa = [block[8 * t : 8 * t + 8] for t in range(tiles)]
+    wa = [block[8 * t : 8 * t + 8, :] for t in range(tiles)]
     wi = [jnp.where(lane == row + 8 * t, 1.0, 0.0).astype(F32) for t in range(tiles)]
-    upper, inverse = [], []
     for t in range(tiles):
         cols = {w: [lanes(wa[w], 8 * t + m) for m in range(8)] for w in range(t, tiles)}
         sc = [[sublanes(cols[t][n], m) if n <= m else None for n in range(8)] for m in range(8)]
@@ -291,8 +375,9 @@
         for m in range(1, 8):
             up = jnp.where(row == m, ua[m], up)
             inv = jnp.where(row == m, ui[m], inv)
-        upper.append(jnp.where(lane >= row + 8 * t, up, 0.0))
-        inverse.append(jnp.where(lane <= row + 8 * t, inv, 0.0))
+        upper[8 * t : 8 * t + 8, :] = jnp.where(lane >= row + 8 * t, up, 0.0)
+        inverse[8 * t : 8 * t + 8, :] = jnp.where(lane <= row + 8 * t, inv, 0.0)
+        after(t)
         if t == tiles - 1:
             break
         ya, yi = [None] * 8, [None] * 8
@@ -308,88 +393,27 @@
                 a = a - cols[w][m] * ya[m]
                 b = b - cols[w][m] * yi[m]
             wa[w], wi[w] = a, b
-    return jnp.concatenate(upper, 0), jnp.concatenate(inverse, 0)
 
 
 ROWS_T = ((1,), (1,))
 PLAIN = ((1,), (0,))
 
 
-def place(maps, base, c, s, r, q, local, read):
-    for u in range(3):
-        a = row_target(maps, c, local(u), r)
-        for m in range(3):
-            b = col_target(maps, c, m, q)
-            t = tile(base, a, b)
-            t[...] = t[...] + read(u, m)
-
-
-def factor_kernel(maps, corner, left, right, front, children, panel, upper, base, pr):
+def finish_kernel(maps, base, arrived, out):
     s, r, q = position()
-    d = {(i, k): corner[i, k] for i in range(NPB) for k in range(i + 1)}
-    for k in range(NPB):
-        up, inv = factor_block(d[k, k])
-        upper[k] = up
-        low = {}
-        for i in range(k + 1, NPB):
-            low[i] = dot(d[i, k], inv, ROWS_T)
-        for i in range(k + 1, NPB):
-            for j in range(k + 1, i + 1):
-                d[i, j] = d[i, j] - dot(low[i], low[j], ROWS_T)
-        mine = left[k].reshape(5 * BS, BS)
-        for i in range(k):
-            mine = mine - dot(panel[:, i * BS : (i + 1) * BS], lows[k, i], ROWS_T)
-        panel[:, k * BS : (k + 1) * BS] = dot(mine, inv, ROWS_T)
-        for n in range(5):
-            other = right[k, n]
-            for i in range(k):
-                other = other - dot(lows[k, i], pr[i * BS : (i + 1) * BS, n * BS : (n + 1) * BS], PLAIN)
-            pr[k * BS : (k + 1) * BS, n * BS : (n + 1) * BS] = dot(inv, other, PLAIN)
-        if k == 0:
-            lows = {}
-        for i in low:
-            lows[i, k] = low[i]
-
-    for a in range(5):
-        rows = slice(a * BS, (a + 1) * BS)
-        base[rows, :] = front[rows, :] - dot(panel[rows, :], pr[...], PLAIN)
-    for c in range(2):
-        place(
-            maps, base, 2 * s + c, s, r, q, lambda u: 2 * u + s,
-            lambda u, m: children[c, pl.ds(pl.multiple_of((2 * u + s) * BS, BS), BS), m * BS : (m + 1) * BS],
-        )
-
-
-def finish_kernel(maps, base, arrived, panel, upper, out):
-    s, r, q = position()
-    dev_row = 8 * s + r
     out[...] = base[...]
     for c in range(2):
-        place(
-            maps, out, 2 * (1 - s) + c, s, r, q, lambda u: 2 * u + s,
-            lambda u, m: arrived[c, u, :, m * BS : (m + 1) * BS],
-        )
-
-    @pl.when(q < NPB)
-    def _():
-        lane = pl.ds(pl.multiple_of(q * BS, BS), BS)
-        out[BS:, :BS] = panel[BS:, lane]
-
-        @pl.when(dev_row > q)
-        def _():
-            out[:BS, :BS] = panel[:BS, lane]
-
-        @pl.when(dev_row == q)
-        def _():
-            out[:BS, :BS] = upper[q].T
-
-    @pl.when(dev_row < NPB)
-    def _():
-        out[:BS, BS:] = jnp.zeros((BS, 4 * BS), F32)
-
-        @pl.when(q > dev_row)
-        def _():
-            out[:BS, :BS] = jnp.zeros((BS, BS), F32)
+        child = 2 * (1 - s) + c
+        for u in range(3):
+            a = row_target(maps, child, 2 * u + s, r)
+            for m in range(3):
+                b = col_target(maps, child, m, q)
+                pivot = ((a == 0) & (8 * s + r < NPB)) | ((b == 0) & (q < NPB))
+
+                @pl.when(jnp.logical_not(pivot))
+                def _():
+                    t = tile(out, a, b)
+                    t[...] = t[...] + arrived[c, u, :, m * BS : (m + 1) * BS]
 
 
 def shape(*dims):
@@ -397,20 +421,30 @@
 
 
 def body(front, children, child_maps):
-    col_send, col_mine, row_send, row_mine, bulk = pl.pallas_call(
+    col_send, col_mine, row_send, row_mine, bulk, assembled = pl.pallas_call(
         prepare_kernel,
-        out_shape=[shape(5, BS, BS)] * 4 + [shape(2, 3, BS, 3 * BS)],
+        out_shape=[shape(5, BS, BS)] * 4 + [shape(2, 3, BS, 3 * BS), shape(5 * BS, 5 * BS)],
         in_specs=[SMEM, VMEM, VMEM],
-        out_specs=[VMEM] * 5,
+        out_specs=[VMEM] * 6,
         name="prepare",
     )(child_maps, front, children)
     dma = pltpu.SemaphoreType.DMA
-    left, right, corner = pl.pallas_call(
-        spread_kernel,
-        out_shape=[shape(NPB, 5, BS, BS), shape(NPB, 5, BS, BS), shape(NPB, NPB, BS, BS)],
-        in_specs=[VMEM] * 4,
-        out_specs=[VMEM] * 3,
+    strips, blocks = pltpu.VMEM((NPB, 5, BS, BS), F32), pltpu.VMEM((NPB, NPB, BS, BS), F32)
+    base, arrived = pl.pallas_call(
+        eliminate_kernel,
+        out_shape=[shape(5 * BS, 5 * BS), shape(2, 3, BS, 3 * BS)],
+        in_specs=[VMEM] * 4 + [ANY, VMEM],
+        out_specs=[VMEM, ANY],
         scratch_shapes=[
+            strips,
+            strips,
+            blocks,
+            blocks,
+            blocks,
+            pltpu.VMEM((NPB, BS, BS), F32),
+            pltpu.VMEM((NPB, BS, BS), F32),
+            pltpu.VMEM((5 * BS, NPB * BS), F32),
+            pltpu.VMEM((NPB * BS, 5 * BS), F32),
             pltpu.VMEM((5, BS, BS), F32),
             pltpu.VMEM((5, BS, BS), F32),
             dma((2, 5)),
@@ -419,28 +453,19 @@
             dma((NPB, 5)),
             dma((NPB, 8, 4)),
             dma((NPB, 8)),
+            dma((2, 3)),
+            dma((2, 3)),
         ],
         compiler_params=pltpu.CompilerParams(collective_id=0, has_side_effects=True),
-        name="spread",
-    )(col_send, col_mine, row_send, row_mine)
-    bulk, corner = lax.optimization_barrier((bulk, corner))
-    arrived = lax.ppermute(bulk, "sub", [(0, 1), (1, 0)])
-    panel, upper, base = pl.pallas_call(
-        factor_kernel,
-        out_shape=[shape(5 * BS, NPB * BS), shape(NPB, BS, BS), shape(5 * BS, 5 * BS)],
-        in_specs=[SMEM] + [VMEM] * 5,
-        out_specs=[VMEM] * 3,
-        scratch_shapes=[pltpu.VMEM((NPB * BS, 5 * BS), F32)],
-        cost_estimate=pl.CostEstimate(flops=10**10, bytes_accessed=10**8, transcendentals=0),
-        name="factor",
-    )(child_maps, corner, left, right, front, children)
+        name="eliminate",
+    )(col_send, col_mine, row_send, row_mine, bulk, assembled)
     return pl.pallas_call(
         finish_kernel,
         out_shape=shape(5 * BS, 5 * BS),
-        in_specs=[SMEM] + [VMEM] * 4,
+        in_specs=[SMEM, VMEM, VMEM],
         out_specs=VMEM,
         name="finish",
-    )(child_maps, base, arrived, panel, upper)
+    )(child_maps, base, arrived)
 
 
 def solution(mesh):

time: 83.2 us -> 104 us (1.25)
  the two profiles are of different devices: /device:TPU:160 before, /device:TPU:144 now
where the time goes in v3:
time: 104 us
  Pallas kernels  104 us (100%)
    pallas_call x1, Pallas kernels, body(): pl.pallas_call(eliminate_kernel, out_shape=[shape(5 * BS, 5 * BS), shape(...  96.7 us
    pallas_call x1, Pallas kernels, body(): pl.pallas_call(prepare_kernel, out_shape=[shape(5, BS, BS)] * 4 + [shape(...  4.24 us
    pallas_call x1, Pallas kernels, body(): pl.pallas_call(finish_kernel, out_shape=shape(5 * BS, 5 * BS), in_specs=[...  3.45 us

profile of v3, /device:TPU:144, one launch (start us, length us, event | category | flops | bytes accessed | tf_op | source)
XLA Modules:
  0.0 104.4 jit_solution(8649989976725345241)
XLA Ops:
  0.0 4.2 %prepare.1 = (f32[5,128,128]{2,1,0:T(8,128)}, f32[5,128,128]{2,1,0:T(8,128)}, f32[5,128,128]{2,1,0:T(8,128)}, f32[5,128,128]{2,1,0:T(8,128)}, f32[2,3,128,384]{3,2,1,0:T(8,128)}, /*index=5*/f32[640,640]{1,0:T(8,128)}) custom-call(s32[4,48]{1,0:T(4,128)} %maps.3, f32[640,640]{1,0:T(8,128)} %front.1, f32[2,768,384]{2,1,0:T(8,128)} %children.1), custom_call_target="tpu_custom_call" | custom-call | tf_op jit(solution)/shard_map/prepare/pallas_call | solution.py:424
  4.2 96.7 %eliminate.1 = (f32[640,640]{1,0:T(8,128)}, f32[2,3,128,384]{3,2,1,0:T(8,128)}) custom-call(f32[5,128,128]{2,1,0:T(8,128)} %get-tuple-element.13.col_send, f32[5,128,128]{2,1,0:T(8,128)} %get-tuple-element.14.col_mine, f32[5,128,128]{2,1,0:T(8,128)} %get-tuple-element.15.row_send, f32[5,128,128]{2,1,0:T(8,128)} %get-tuple-element.16.row_mine, ...), custom_call_target="tpu_custom_call" | custom-call | tf_op jit(solution)/shard_map/eliminate/pallas_call | solution.py:433
  100.9 3.5 %finish.1 = f32[640,640]{1,0:T(8,128)} custom-call(s32[4,48]{1,0:T(4,128)} %maps.3, f32[640,640]{1,0:T(8,128)} %get-tuple-element.19.base, f32[2,3,128,384]{3,2,1,0:T(8,128)} %get-tuple-element.20.arrived), custom_call_target="tpu_custom_call" | custom-call | tf_op jit(solution)/shard_map/finish/pallas_call | solution.py:462

commit v4 on v0

v4 whole, which is shorter than its diff:
```python
import jax
import jax.numpy as jnp
from jax import lax
from jax.experimental import pallas as pl
from jax.experimental.pallas import tpu as pltpu
from jax.sharding import PartitionSpec as P

BS = 128
NPB = 3
LEAF = 8
F32 = jnp.float32
MESH = pl.DeviceIdType.MESH
HIGHEST = lax.Precision.HIGHEST
VMEM = pl.BlockSpec(memory_space=pltpu.VMEM)
SMEM = pl.BlockSpec(memory_space=pltpu.SMEM)
ANY = pl.BlockSpec(memory_space=pl.ANY)
SOURCE = ((0, 0, 1), (2, 0, -1), (0, 1, 1))
HALF = BS // 2
PIECES = 12
EARLY = 4
ROW_DELAY = 3


def position():
    return lax.axis_index("sub"), lax.axis_index("row"), lax.axis_index("col")


def dot(a, b, dims):
    return lax.dot_general(a, b, (dims, ((), ())), precision=HIGHEST, preferred_element_type=F32)


def chosen(targets, want, values):
    result = jnp.zeros_like(values[0])
    for target, value in zip(targets, values):
        result = jnp.where(target == want, value, result)
    return result


def placed(rows, cols, read, down, across):
    total = {}
    for c in range(2):
        strips = [[read(c, u, m) for m in range(3)] for u in range(3)]
        for b in across:
            part = [chosen(cols[c], b, strips[u]) for u in range(3)]
            for a in down:
                value = chosen(rows[c], a, part)
                total[a, b] = total[a, b] + value if c else value
    return total


def span(start, size):
    return pl.ds(pl.multiple_of(start * size, size), size)


def lanes(v, j):
    return jnp.take_along_axis(v, jnp.full((8, BS), j, jnp.int32), axis=1)


def sublanes(v, i):
    return jnp.broadcast_to(v[i : i + 1, :], (8, BS))


def factor_block(block, upper, inverse, after):
    row = lax.broadcasted_iota(jnp.int32, (8, BS), 0)
    lane = lax.broadcasted_iota(jnp.int32, (8, BS), 1)
    tiles = BS // LEAF
    wa = [block[8 * t : 8 * t + 8, :] for t in range(tiles)]
    wi = [jnp.where(lane == row + 8 * t, 1.0, 0.0).astype(F32) for t in range(tiles)]
    for t in range(tiles):
        cols = {w: [lanes(wa[w], 8 * t + m) for m in range(8)] for w in range(t, tiles)}
        sc = [[sublanes(cols[t][n], m) if n <= m else None for n in range(8)] for m in range(8)]
        low = [[None] * 8 for _ in range(8)]
        rs, ua, ui = [None] * 8, [None] * 8, [None] * 8
        for m in range(8):
            rs[m] = lax.rsqrt(sc[m][m])
            for i in range(m + 1, 8):
                low[i][m] = sc[i][m] * rs[m]
            for i in range(m + 1, 8):
                for j in range(m + 1, i + 1):
                    sc[i][j] = sc[i][j] - low[i][m] * low[j][m]
            ga, gi = sublanes(wa[t], m), sublanes(wi[t], m)
            for n in range(m):
                ga = ga - low[m][n] * ua[n]
                gi = gi - low[m][n] * ui[n]
            ua[m], ui[m] = ga * rs[m], gi * rs[m]
        up, inv = ua[0], ui[0]
        for m in range(1, 8):
            up = jnp.where(row == m, ua[m], up)
            inv = jnp.where(row == m, ui[m], inv)
        upper[8 * t : 8 * t + 8, :] = jnp.where(lane >= row + 8 * t, up, 0.0)
        inverse[8 * t : 8 * t + 8, :] = jnp.where(lane <= row + 8 * t, inv, 0.0)
        after(t)
        if t == tiles - 1:
            break
        ya, yi = [None] * 8, [None] * 8
        for m in reversed(range(8)):
            a, b = ua[m], ui[m]
            for n in range(m + 1, 8):
                a = a - low[n][m] * ya[n]
                b = b - low[n][m] * yi[n]
            ya[m], yi[m] = a * rs[m], b * rs[m]
        for w in range(t + 1, tiles):
            a, b = wa[w], wi[w]
            for m in range(8):
                a = a - cols[w][m] * ya[m]
                b = b - cols[w][m] * yi[m]
            wa[w], wi[w] = a, b


ROWS_T = ((1,), (1,))
PLAIN = ((1,), (0,))


def kernel(maps, front, children, out, kids, arrived, left, right, corner, work, lows, inverses, uppers, panel, pr,
           col_send, col_mine, col_recv, row_send, row_mine, row_recv,
           fs, xs, xr, zs, zr, ys, yr, ls, cx, cy, cb, cr, br, ps, pq):
    s, r, q = position()
    dev_row = 8 * s + r
    x, y, z, core = 2 * lax.rem(r, 2) + s, r // 2, q // 2, lax.rem(q, 2)

    def at_x(d):
        nx = lax.rem(x + 4 + d, 4)
        return (lax.rem(nx, 2), 2 * y + nx // 2, q)

    def at_y(d):
        return (s, 2 * lax.rem(y + 4 + d, 4) + lax.rem(r, 2), q)

    def at_z(d, to_core=core):
        return (s, r, 2 * lax.rem(z + 8 + d, 8) + to_core)

    sibling = (s, r, 2 * z + 1 - core)
    partner = (1 - s, r, q)

    barrier = pltpu.get_barrier_semaphore()
    peers = [at_x(d) for d in (1, 2, 3)] + [at_y(d) for d in (1, 2, 3)]
    peers += [at_z(d, c) for d in range(1, 8) for c in range(2)] + [sibling]
    for peer in peers:
        pl.semaphore_signal(barrier, inc=1, device_id=peer, device_id_type=MESH)
    fetch = [pltpu.make_async_copy(children.at[c], kids.at[c], fs.at[c]) for c in range(2)]
    fetch.append(pltpu.make_async_copy(front, out, fs.at[2]))
    for f in fetch:
        f.start()

    def copy(src, dst, send, recv, device):
        return pltpu.make_async_remote_copy(
            src_ref=src, dst_ref=dst, send_sem=send, recv_sem=recv, device_id=device, device_id_type=MESH
        )

    def rows_of(child, side):
        return [maps[child, (2 * u + side) * 8 + r] // 16 for u in range(3)]

    def cols_of(child):
        return [maps[child, m * 16 + q] // 16 for m in range(3)]

    mine = [(2 * s + c) for c in range(2)]
    cols = [cols_of(child) for child in mine]
    kept = [rows_of(child, s) for child in mine]
    given = [rows_of(child, 1 - s) for child in mine]

    def strips(body):
        @pl.loop(0, BS // 8)
        def _(i):
            body(lambda a: pl.ds(pl.multiple_of(a * BS + 8 * i, 8), 8))

    def own(at, side):
        return lambda c, u, m: kids[c, at(2 * u + side), m * BS : (m + 1) * BS]

    for f in fetch:
        f.wait()

    @pl.when(q < NPB)
    def _():
        @strips
        def _(at):
            sent = placed(given, cols, own(at, 1 - s), range(5), [0])
            stay = placed(kept, cols, own(at, s), range(5), [0])
            for n in range(5):
                col_send[n, at(0), :] = sent[n, 0]
                col_mine[n, at(0), :] = out[at(n), :BS] + stay[n, 0]

    @pl.when(r < NPB)
    def _():
        @strips
        def _(at):
            first = placed([rows_of(child, 0) for child in mine], cols, own(at, 0), [0], range(5))
            for n in range(5):
                row_send[n, at(0), :] = first[0, n]
                row_mine[n, at(0), :] = out[at(0), n * BS : (n + 1) * BS] + first[0, n]

    pl.semaphore_wait(barrier, len(peers))

    def col_copy(n):
        return copy(col_send.at[n], col_recv.at[n], xs.at[0, n], xr.at[0, n], partner)

    def row_copy(n):
        return copy(row_send.at[n], row_recv.at[n], xs.at[1, n], xr.at[1, n], partner)

    def exchange(act):
        @pl.when(q < NPB)
        def _():
            for n in range(5):
                act(col_copy(n))

        @pl.when((r < NPB) & (s == 1))
        def _():
            for n in range(5):
                act(row_copy(n))

    def piece(j):
        c, u, half = j // 6, lax.rem(j // 2, 3), lax.rem(j, 2)
        return copy(
            kids.at[c, pl.ds(pl.multiple_of((2 * u + 1 - s) * BS + half * HALF, HALF), HALF), :],
            arrived.at[c, u, pl.ds(pl.multiple_of(half * HALF, HALF), HALF), :],
            ps.at[j], pq.at[j], partner,
        )

    patient = (s == 0) & (y < 2)
    exchange(lambda c: c.start())

    @pl.when(jnp.logical_not(patient))
    def _():
        @pl.loop(0, PIECES)
        def _(j):
            piece(j).start()

    def add(rows, cols, read):
        @strips
        def _(at):
            total = placed(rows, cols, read(at), range(5), range(5))
            for a in range(5):
                for b in range(5):
                    lanes_b = slice(b * BS, (b + 1) * BS)
                    out[at(a), lanes_b] = out[at(a), lanes_b] + total[a, b]

    add(kept, cols, lambda at: own(at, s))

    line = []
    for k in range(NPB):
        dz = lax.rem(z - k // 2 + 8, 8)
        on = core == k % 2
        hops = jnp.where(dz <= 4, dz, 8 - dz) + jnp.where(on, 0, 1)
        line.append((on & (dz <= 3), on & ((dz == 0) | (dz >= 6)), on, hops))
    z_up, z_down = at_z(1), at_z(-1)

    def line_sends(k, n, act):
        up, down, on, _ = line[k]
        here = left.at[k, n]

        @pl.when(up)
        def _():
            act(copy(here, here, zs.at[k, n, 0], zr.at[k, n], z_up))

        @pl.when(down)
        def _():
            act(copy(here, here, zs.at[k, n, 1], zr.at[k, n], z_down))

        @pl.when(on)
        def _():
            act(copy(here, here, zs.at[k, n, 2], zr.at[k, n], sibling))

    def col_make(k, n):
        col_copy(n).wait_recv()
        left[k, n] = col_mine[n] + col_recv[n]

    def line_step(k, n):
        @pl.when((q == k) & (n > 0))
        def _():
            col_make(k, n)

        @pl.when(q != k)
        def _():
            copy(left.at[k, n], left.at[k, n], zs.at[k, n, 0], zr.at[k, n], sibling).wait_recv()

        line_sends(k, n, lambda c: c.start())

    plane = []
    for xi, yi, g in SOURCE:
        dx, dy = lax.rem(x - xi + 4, 4), lax.rem(g * (y - yi) + 4, 4)
        hops = jnp.where(dx == 3, 1, dx) + jnp.where(dy == 3, 1, dy)
        plane.append(((dy == 0) & (dx <= 1), (dy == 0) & (dx == 0), dy <= 1, dy == 0, hops))
    x_up, x_down, y_up, y_down = at_x(1), at_x(-1), at_y(1), at_y(-1)

    def plane_sends(i, n, act):
        g = SOURCE[i][2]
        here = right.at[i, n]
        targets = (x_up, x_down, y_up if g > 0 else y_down, y_down if g > 0 else y_up)
        for way in range(4):

            @pl.when(plane[i][way])
            def _():
                act(copy(here, here, ys.at[i, n, way], yr.at[i, n], targets[way]))

    def plane_step(i, n):
        @pl.when(plane[i][4] == 0)
        def _():
            row_copy(n).wait_recv()
            right[i, n] = row_mine[n] + row_recv[n]

        @pl.when(plane[i][4] > 0)
        def _():
            copy(right.at[i, n], right.at[i, n], ys.at[i, n, 0], yr.at[i, n], sibling).wait_recv()

        plane_sends(i, n, lambda c: c.start())

    corners = [(i, k) for i in range(NPB) for k in range(i + 1)]
    my_half = span(core, HALF)
    far_z = (4, 3, 5, 2, 6, 1, 7)

    def corner_stage(i):
        xi, yi, _ = SOURCE[i]
        at_line = dev_row == i
        return at_line, y == yi

    def corner_line(i, k, act):
        for d in range(7):
            for c in range(2):
                part = corner.at[i, k, c * HALF : (c + 1) * HALF, :]
                act(copy(part, part, ls.at[2 * d + c], cr.at[i, k], at_z(far_z[d], c)))
        part = corner.at[i, k, span(1 - core, HALF), :]
        act(copy(part, part, ls.at[14], cr.at[i, k], sibling))

    def corner_sends(i, k, act):
        at_line, at_row = corner_stage(i)
        part = corner.at[i, k, my_half, :]

        @pl.when(at_line & (q == k))
        def _():
            corner_line(i, k, act)

        @pl.when(at_line)
        def _():
            for d in (2, 1, 3):
                act(copy(part, part, cx.at[i, k, d], cr.at[i, k], at_x(d)))

        @pl.when(at_row)
        def _():
            for d in (2, 1, 3):
                act(copy(part, part, cy.at[i, k, d], cr.at[i, k], at_y(d)))

        @pl.when(jnp.logical_not(at_line & (q == k ^ 1)))
        def _():
            act(copy(part, part, cb.at[i, k], br.at[i, k], sibling))

    def corner_step(i, k, stage):
        at_line, at_row = corner_stage(i)
        mine_now = (at_line & (q == k), at_line & (q != k), at_row & jnp.logical_not(at_line), jnp.logical_not(at_row))

        @pl.when(mine_now[stage])
        def _():
            if stage == 0:
                corner[i, k] = left[k, 0]
            else:
                part = corner.at[i, k, my_half, :]
                copy(part, part, cb.at[i, k], cr.at[i, k], sibling).wait_recv()
            corner_sends(i, k, lambda c: c.start())

    for k in range(NPB):

        @pl.when(q == k)
        def _():
            col_make(k, 0)

    def rest(slot):
        for k in range(NPB):
            n = slot - line[k][3]

            @pl.when((n >= 0) & (n < 5))
            def _():
                line_step(k, n)

        for i in range(NPB):
            n = slot - plane[i][4] - ROW_DELAY

            @pl.when((n >= 0) & (n < 5))
            def _():
                plane_step(i, n)

        if isinstance(slot, int) and slot < ROW_DELAY:
            return

        @pl.when(patient)
        def _():
            piece(slot - ROW_DELAY).start()

    for slot in range(EARLY):
        for i, k in corners:
            corner_step(i, k, slot)
        rest(slot)
    for i, k in corners:
        other = corner.at[i, k, span(1 - core, HALF), :]

        @pl.when(jnp.logical_not((dev_row == i) & (q == k)))
        def _():
            copy(other, other, cb.at[i, k], br.at[i, k], sibling).wait_recv()

        work[i, k] = corner[i, k]

    @pl.loop(0, NPB)
    def _(k):
        def after(t):
            if t % 5 == 4:
                rest(EARLY + 3 * k + t // 5)

        factor_block(work.at[k, k], uppers.at[k], inverses.at[k], after)
        inv = inverses[k]
        for i in range(1, NPB):

            @pl.when(i > k)
            def _():
                lows[i, k] = dot(work[i, k], inv, ROWS_T)

        for i in range(1, NPB):
            for j in range(1, i + 1):

                @pl.when(j > k)
                def _():
                    work[i, j] = work[i, j] - dot(lows[i, k], lows[j, k], ROWS_T)

    @pl.loop(EARLY + 9, ROW_DELAY + PIECES)
    def _(slot):
        rest(slot)

    for k in range(NPB):
        inv = inverses[k]
        own = left[k].reshape(5 * BS, BS)
        for i in range(k):
            own = own - dot(panel[:, i * BS : (i + 1) * BS], lows[k, i], ROWS_T)
        panel[:, k * BS : (k + 1) * BS] = dot(own, inv, ROWS_T)
        for n in range(5):
            other = right[k, n]
            for i in range(k):
                other = other - dot(lows[k, i], pr[i * BS : (i + 1) * BS, n * BS : (n + 1) * BS], PLAIN)
            pr[k * BS : (k + 1) * BS, n * BS : (n + 1) * BS] = dot(inv, other, PLAIN)

    for a in range(5):
        rows = slice(a * BS, (a + 1) * BS)
        out[rows, :] = out[rows, :] - dot(panel[rows, :], pr[...], PLAIN)

    @pl.loop(0, PIECES)
    def _(j):
        piece(j).wait()

    theirs = [2 * (1 - s) + c for c in range(2)]
    add(
        [rows_of(child, s) for child in theirs],
        [cols_of(child) for child in theirs],
        lambda at: lambda c, u, m: arrived[c, u, at(0), m * BS : (m + 1) * BS],
    )

    for k in range(NPB):

        @pl.when(q == k)
        def _():
            out[BS:, :BS] = panel[BS:, k * BS : (k + 1) * BS]

            @pl.when(dev_row > k)
            def _():
                out[:BS, :BS] = panel[:BS, k * BS : (k + 1) * BS]

            @pl.when(dev_row == k)
            def _():
                out[:BS, :BS] = uppers[k].T

    @pl.when(dev_row < NPB)
    def _():
        out[:BS, BS:] = jnp.zeros((BS, 4 * BS), F32)

        @pl.when(q > dev_row)
        def _():
            out[:BS, :BS] = jnp.zeros((BS, BS), F32)

    exchange(lambda c: c.wait_send())
    for i, k in corners:
        corner_sends(i, k, lambda c: c.wait_send())

    @pl.loop(0, 5)
    def _(n):
        for k in range(NPB):
            line_sends(k, n, lambda c: c.wait_send())
        for i in range(NPB):
            plane_sends(i, n, lambda c: c.wait_send())


def body(front, children, child_maps):
    dma = pltpu.SemaphoreType.DMA

    def vmem(*dims):
        return pltpu.VMEM(dims, F32)

    return pl.pallas_call(
        kernel,
        out_shape=jax.ShapeDtypeStruct((5 * BS, 5 * BS), F32),
        in_specs=[SMEM, ANY, ANY],
        out_specs=VMEM,
        scratch_shapes=[
            vmem(2, 6 * BS, 3 * BS),
            vmem(2, 3, BS, 3 * BS),
            vmem(NPB, 5, BS, BS),
            vmem(NPB, 5, BS, BS),
            vmem(NPB, NPB, BS, BS),
            vmem(NPB, NPB, BS, BS),
            vmem(NPB, NPB, BS, BS),
            vmem(NPB, BS, BS),
            vmem(NPB, BS, BS),
            vmem(5 * BS, NPB * BS),
            vmem(NPB * BS, 5 * BS),
        ]
        + [vmem(5, BS, BS)] * 6
        + [
            dma((3,)),
            dma((2, 5)),
            dma((2, 5)),
            dma((NPB, 5, 3)),
            dma((NPB, 5)),
            dma((NPB, 5, 4)),
            dma((NPB, 5)),
            dma((15,)),
            dma((NPB, NPB, 4)),
            dma((NPB, NPB, 4)),
            dma((NPB, NPB)),
            dma((NPB, NPB)),
            dma((NPB, NPB)),
            dma((PIECES,)),
            dma((PIECES,)),
        ],
        compiler_params=pltpu.CompilerParams(collective_id=0, has_side_effects=True),
        name="front",
    )(child_maps, front, children)


def solution(mesh):
    return jax.shard_map(
        body,
        mesh=mesh,
        in_specs=(P(("sub", "row"), "col"), P("sub", "row", "col"), P()),
        out_specs=P(("sub", "row"), "col"),
        check_vma=False,
    )
```

time: 1430 us -> 75.2 us (0.05)
  the two profiles are of different devices: /device:TPU:160 before, /device:TPU:80 now
where the time goes in v4:
time: 75.2 us; the launch traced here: 75.1 us
  Pallas kernels  72.4 us (96%)
  local copies, waits for them, and re-layouts  2.7 us (4%)
    pallas_call x1, Pallas kernels, body(): pl.pallas_call(kernel, out_shape=jax.ShapeDtypeStruct((5 * BS, 5 * BS), F...  72.4 us
    unnamed x1, local copies, waits for them, and re-layouts  2.7 us

profile of v4, /device:TPU:80, one launch (start us, length us, event | category | flops | bytes accessed | tf_op | source)
XLA Modules:
  0.0 75.1 jit_solution(7895143251321524773)
XLA Ops:
  0.0 72.4 %front.2 = f32[640,640]{1,0:T(8,128)} custom-call(s32[4,48]{1,0:T(4,128)} %maps.1, f32[640,640]{1,0:T(8,128)} %front.3, f32[2,768,384]{2,1,0:T(8,128)} %children.1), custom_call_target="tpu_custom_call" | custom-call | tf_op jit(solution)/shard_map/front/pallas_call | solution.py:490
  72.4 2.7 %copy.5 = f32[640,640]{1,0:T(8,128)} copy(f32[640,640]{1,0:T(8,128)} %front.2) | data formatting | bytes 3276800

commit v5 on v4

--- a/solution.py
+++ b/solution.py
@@ -8,17 +8,16 @@
 BS = 128
 NPB = 3
 LEAF = 8
+Y_AT = (0, 4)
+Z_AT = (1, 4)
 F32 = jnp.float32
 MESH = pl.DeviceIdType.MESH
 HIGHEST = lax.Precision.HIGHEST
 VMEM = pl.BlockSpec(memory_space=pltpu.VMEM)
 SMEM = pl.BlockSpec(memory_space=pltpu.SMEM)
 ANY = pl.BlockSpec(memory_space=pl.ANY)
-SOURCE = ((0, 0, 1), (2, 0, -1), (0, 1, 1))
+SOURCE = ((0, 0), (2, 0), (0, 1))
 HALF = BS // 2
-PIECES = 12
-EARLY = 4
-ROW_DELAY = 3
 
 
 def position():
@@ -112,8 +111,8 @@
 
 
 def kernel(maps, front, children, out, kids, arrived, left, right, corner, work, lows, inverses, uppers, panel, pr,
-           col_send, col_mine, col_recv, row_send, row_mine, row_recv,
-           fs, xs, xr, zs, zr, ys, yr, ls, cx, cy, cb, cr, br, ps, pq):
+           col_send, col_mine, row_send, row_mine, first_recv, line_in, plane_in,
+           fs, xs, sl, sp, rl, rp, gs, gr, hs, hr, ws, wr, bs, br, ls, cx, cy, cb, cr, cbr, ps, pq):
     s, r, q = position()
     dev_row = 8 * s + r
     x, y, z, core = 2 * lax.rem(r, 2) + s, r // 2, q // 2, lax.rem(q, 2)
@@ -132,8 +131,18 @@
     partner = (1 - s, r, q)
 
     barrier = pltpu.get_barrier_semaphore()
-    peers = [at_x(d) for d in (1, 2, 3)] + [at_y(d) for d in (1, 2, 3)]
-    peers += [at_z(d, c) for d in range(1, 8) for c in range(2)] + [sibling]
+    plane_peers = [(dx, dy) for dx in range(4) for dy in range(4)]
+    line_peers = [(dz, c) for dz in range(8) for c in range(2)]
+
+    def in_line(side, dz, c):
+        return (side, r, 2 * lax.rem(z + dz, 8) + lax.rem(core + c, 2))
+
+    def in_plane(dx, dy):
+        nx = lax.rem(x + dx, 4)
+        return (lax.rem(nx, 2), 2 * lax.rem(y + dy, 4) + nx // 2, q)
+
+    peers = [in_line(s, *p) for p in line_peers[1:]] + [in_line(1 - s, *p) for p in line_peers[1:]]
+    peers += [in_plane(*p) for p in plane_peers[1:]]
     for peer in peers:
         pl.semaphore_signal(barrier, inc=1, device_id=peer, device_id_type=MESH)
     fetch = [pltpu.make_async_copy(children.at[c], kids.at[c], fs.at[c]) for c in range(2)]
@@ -189,39 +198,94 @@
 
     pl.semaphore_wait(barrier, len(peers))
 
-    def col_copy(n):
-        return copy(col_send.at[n], col_recv.at[n], xs.at[0, n], xr.at[0, n], partner)
-
-    def row_copy(n):
-        return copy(row_send.at[n], row_recv.at[n], xs.at[1, n], xr.at[1, n], partner)
-
-    def exchange(act):
-        @pl.when(q < NPB)
-        def _():
-            for n in range(5):
-                act(col_copy(n))
-
-        @pl.when((r < NPB) & (s == 1))
-        def _():
-            for n in range(5):
-                act(row_copy(n))
-
-    def piece(j):
-        c, u, half = j // 6, lax.rem(j // 2, 3), lax.rem(j, 2)
-        return copy(
-            kids.at[c, pl.ds(pl.multiple_of((2 * u + 1 - s) * BS + half * HALF, HALF), HALF), :],
-            arrived.at[c, u, pl.ds(pl.multiple_of(half * HALF, HALF), HALF), :],
-            ps.at[j], pq.at[j], partner,
-        )
-
-    patient = (s == 0) & (y < 2)
-    exchange(lambda c: c.start())
-
-    @pl.when(jnp.logical_not(patient))
+    def first_copy():
+        return copy(col_send.at[0], first_recv, xs.at[0], xs.at[1], partner)
+
+    first_on = (r < NPB) & (q < NPB)
+
+    @pl.when(first_on & (s == 1))
     def _():
-        @pl.loop(0, PIECES)
-        def _(j):
-            piece(j).start()
+        first_copy().start()
+
+    def line_rows(dz, c):
+        return pl.ds(pl.multiple_of(HALF * lax.rem(core + c, 2) + 8 * lax.rem(z + dz, 8), 8), 8)
+
+    def plane_rows(dx, dy):
+        return pl.ds(pl.multiple_of(32 * lax.rem(y + dy, 4) + 8 * lax.rem(x + dx, 4), 8), 8)
+
+    own_line, own_plane = line_rows(0, 0), plane_rows(0, 0)
+
+    def scatter(act):
+        for k in range(NPB):
+
+            @pl.when(q == k)
+            def _():
+                for j, p in enumerate(line_peers):
+                    rows = line_rows(*p)
+                    act(copy(col_send.at[:, rows], line_in.at[k, 1], sl.at[1, j], rl.at[k, 1], in_line(1 - s, *p)))
+                    if j:
+                        act(copy(col_mine.at[:, rows], line_in.at[k, 0], sl.at[0, j], rl.at[k, 0], in_line(s, *p)))
+
+        for i in range(NPB):
+            for side, held in ((0, row_mine), (1, row_send)):
+
+                @pl.when((r == i) & (s == side))
+                def _():
+                    for j, p in enumerate(plane_peers):
+                        if j:
+                            rows = plane_rows(*p)
+                            act(copy(held.at[:, rows], plane_in.at[i, side], sp.at[j], rp.at[i, side], in_plane(*p)))
+
+    def gather_sum():
+        for k in range(NPB):
+            copy(line_in.at[k, 1], line_in.at[k, 1], sl.at[1, 0], rl.at[k, 1], sibling).wait_recv()
+
+            @pl.when(q == k)
+            def _():
+                left[k, :, own_line, :] = col_mine[:, own_line, :] + line_in[k, 1]
+
+            @pl.when(q != k)
+            def _():
+                copy(line_in.at[k, 0], line_in.at[k, 0], sl.at[0, 0], rl.at[k, 0], sibling).wait_recv()
+                left[k, :, own_line, :] = line_in[k, 0] + line_in[k, 1]
+
+        for i in range(NPB):
+            for side, held in ((0, row_mine), (1, row_send)):
+                holder = (r == i) & (s == side)
+
+                @pl.when(holder)
+                def _():
+                    plane_in[i, side] = held[:, own_plane, :]
+
+                @pl.when(jnp.logical_not(holder))
+                def _():
+                    copy(plane_in.at[i, side], plane_in.at[i, side], sp.at[0], rp.at[i, side], sibling).wait_recv()
+
+            right[i, :, own_plane, :] = plane_in[i, 0] + plane_in[i, 1]
+
+    def along_z(act):
+        here = left.at[:, :, own_line]
+        for d in (4, 3, 5, 2, 6, 1, 7):
+            act(copy(here, here, gs.at[d], gr.at[d], at_z(d)))
+
+    def along_x(act):
+        here = right.at[:, :, own_plane]
+        for d in (2, 1, 3):
+            act(copy(here, here, hs.at[d], hr.at[d], at_x(d)))
+
+    def along_y(act):
+        here = right.at[:, :, span(y, 32)]
+        for d in (2, 1, 3):
+            act(copy(here, here, ws.at[d], wr.at[d], at_y(d)))
+
+    def to_sibling(act):
+        here = left.at[:, :, span(core, HALF)]
+        act(copy(here, here, bs.at[0], br.at[0], sibling))
+
+    def pieces(act):
+        for c in range(2):
+            for u in range(3):
+                act(copy(kids.at[c, span(2 * u + 1 - s, BS), :], arrived.at[c, u], ps.at[c, u], pq.at[c, u], partner))
 
     def add(rows, cols, read):
         @strips
@@ -234,80 +298,12 @@
 
     add(kept, cols, lambda at: own(at, s))
 
-    line = []
-    for k in range(NPB):
-        dz = lax.rem(z - k // 2 + 8, 8)
-        on = core == k % 2
-        hops = jnp.where(dz <= 4, dz, 8 - dz) + jnp.where(on, 0, 1)
-        line.append((on & (dz <= 3), on & ((dz == 0) | (dz >= 6)), on, hops))
-    z_up, z_down = at_z(1), at_z(-1)
-
-    def line_sends(k, n, act):
-        up, down, on, _ = line[k]
-        here = left.at[k, n]
-
-        @pl.when(up)
-        def _():
-            act(copy(here, here, zs.at[k, n, 0], zr.at[k, n], z_up))
-
-        @pl.when(down)
-        def _():
-            act(copy(here, here, zs.at[k, n, 1], zr.at[k, n], z_down))
-
-        @pl.when(on)
-        def _():
-            act(copy(here, here, zs.at[k, n, 2], zr.at[k, n], sibling))
-
-    def col_make(k, n):
-        col_copy(n).wait_recv()
-        left[k, n] = col_mine[n] + col_recv[n]
-
-    def line_step(k, n):
-        @pl.when((q == k) & (n > 0))
-        def _():
-            col_make(k, n)
-
-        @pl.when(q != k)
-        def _():
-            copy(left.at[k, n], left.at[k, n], zs.at[k, n, 0], zr.at[k, n], sibling).wait_recv()
-
-        line_sends(k, n, lambda c: c.start())
-
-    plane = []
-    for xi, yi, g in SOURCE:
-        dx, dy = lax.rem(x - xi + 4, 4), lax.rem(g * (y - yi) + 4, 4)
-        hops = jnp.where(dx == 3, 1, dx) + jnp.where(dy == 3, 1, dy)
-        plane.append(((dy == 0) & (dx <= 1), (dy == 0) & (dx == 0), dy <= 1, dy == 0, hops))
-    x_up, x_down, y_up, y_down = at_x(1), at_x(-1), at_y(1), at_y(-1)
-
-    def plane_sends(i, n, act):
-        g = SOURCE[i][2]
-        here = right.at[i, n]
-        targets = (x_up, x_down, y_up if g > 0 else y_down, y_down if g > 0 else y_up)
-        for way in range(4):
-
-            @pl.when(plane[i][way])
-            def _():
-                act(copy(here, here, ys.at[i, n, way], yr.at[i, n], targets[way]))
-
-    def plane_step(i, n):
-        @pl.when(plane[i][4] == 0)
-        def _():
-            row_copy(n).wait_recv()
-            right[i, n] = row_mine[n] + row_recv[n]
-
-        @pl.when(plane[i][4] > 0)
-        def _():
-            copy(right.at[i, n], right.at[i, n], ys.at[i, n, 0], yr.at[i, n], sibling).wait_recv()
-
-        plane_sends(i, n, lambda c: c.start())
-
     corners = [(i, k) for i in range(NPB) for k in range(i + 1)]
     my_half = span(core, HALF)
     far_z = (4, 3, 5, 2, 6, 1, 7)
 
     def corner_stage(i):
-        xi, yi, _ = SOURCE[i]
+        _, yi = SOURCE[i]
         at_line = dev_row == i
         return at_line, y == yi
 
@@ -339,7 +335,7 @@
 
         @pl.when(jnp.logical_not(at_line & (q == k ^ 1)))
         def _():
-            act(copy(part, part, cb.at[i, k], br.at[i, k], sibling))
+            act(copy(part, part, cb.at[i, k], cbr.at[i, k], sibling))
 
     def corner_step(i, k, stage):
         at_line, at_row = corner_stage(i)
@@ -348,58 +344,51 @@
         @pl.when(mine_now[stage])
         def _():
             if stage == 0:
-                corner[i, k] = left[k, 0]
+                first_copy().wait_recv()
+                corner[i, k] = col_mine[0] + first_recv[...]
             else:
                 part = corner.at[i, k, my_half, :]
                 copy(part, part, cb.at[i, k], cr.at[i, k], sibling).wait_recv()
             corner_sends(i, k, lambda c: c.start())
 
-    for k in range(NPB):
-
-        @pl.when(q == k)
-        def _():
-            col_make(k, 0)
-
-    def rest(slot):
-        for k in range(NPB):
-            n = slot - line[k][3]
-
-            @pl.when((n >= 0) & (n < 5))
-            def _():
-                line_step(k, n)
-
-        for i in range(NPB):
-            n = slot - plane[i][4] - ROW_DELAY
-
-            @pl.when((n >= 0) & (n < 5))
-            def _():
-                plane_step(i, n)
-
-        if isinstance(slot, int) and slot < ROW_DELAY:
-            return
-
-        @pl.when(patient)
-        def _():
-            piece(slot - ROW_DELAY).start()
-
-    for slot in range(EARLY):
+    @pl.when(first_on & (s == 0) & (q > r))
+    def _():
+        first_copy().wait_recv()
+
+    for stage in range(4):
         for i, k in corners:
-            corner_step(i, k, slot)
-        rest(slot)
+            corner_step(i, k, stage)
+        if stage == 0:
+            scatter(lambda c: c.start())
+    gather_sum()
+    along_x(lambda c: c.start())
+    along_z(lambda c: c.start())
+    pieces(lambda c: c.start())
     for i, k in corners:
         other = corner.at[i, k, span(1 - core, HALF), :]
 
         @pl.when(jnp.logical_not((dev_row == i) & (q == k)))
         def _():
-            copy(other, other, cb.at[i, k], br.at[i, k], sibling).wait_recv()
+            copy(other, other, cb.at[i, k], cbr.at[i, k], sibling).wait_recv()
 
         work[i, k] = corner[i, k]
 
     @pl.loop(0, NPB)
     def _(k):
         def after(t):
-            if t % 5 == 4:
-                rest(EARLY + 3 * k + t // 5)
+            if t == Y_AT[1]:
+
+                @pl.when(k == Y_AT[0])
+                def _():
+                    along_x(lambda c: c.wait_recv())
+                    along_y(lambda c: c.start())
+
+            if t == Z_AT[1]:
+
+                @pl.when(k == Z_AT[0])
+                def _():
+                    along_z(lambda c: c.wait_recv())
+                    to_sibling(lambda c: c.start())
 
         factor_block(work.at[k, k], uppers.at[k], inverses.at[k], after)
         inv = inverses[k]
@@ -416,9 +405,8 @@
                 def _():
                     work[i, j] = work[i, j] - dot(lows[i, k], lows[j, k], ROWS_T)
 
-    @pl.loop(EARLY + 9, ROW_DELAY + PIECES)
-    def _(slot):
-        rest(slot)
+    along_y(lambda c: c.wait_recv())
+    to_sibling(lambda c: c.wait_recv())
 
     for k in range(NPB):
         inv = inverses[k]
@@ -436,9 +424,7 @@
         rows = slice(a * BS, (a + 1) * BS)
         out[rows, :] = out[rows, :] - dot(panel[rows, :], pr[...], PLAIN)
 
-    @pl.loop(0, PIECES)
-    def _(j):
-        piece(j).wait()
+    pieces(lambda c: c.wait())
 
     theirs = [2 * (1 - s) + c for c in range(2)]
     add(
@@ -461,25 +447,16 @@
             def _():
                 out[:BS, :BS] = uppers[k].T
 
-    @pl.when(dev_row < NPB)
+    @pl.when(first_on & (s == 1))
     def _():
-        out[:BS, BS:] = jnp.zeros((BS, 4 * BS), F32)
-
-        @pl.when(q > dev_row)
-        def _():
-            out[:BS, :BS] = jnp.zeros((BS, BS), F32)
-
-    exchange(lambda c: c.wait_send())
+        first_copy().wait_send()
+
+    scatter(lambda c: c.wait_send())
+    for act in (along_x, along_y, along_z, to_sibling):
+        act(lambda c: c.wait_send())
     for i, k in corners:
         corner_sends(i, k, lambda c: c.wait_send())
 
-    @pl.loop(0, 5)
-    def _(n):
-        for k in range(NPB):
-            line_sends(k, n, lambda c: c.wait_send())
-        for i in range(NPB):
-            plane_sends(i, n, lambda c: c.wait_send())
-
 
 def body(front, children, child_maps):
     dma = pltpu.SemaphoreType.DMA
@@ -487,7 +464,7 @@
     def vmem(*dims):
         return pltpu.VMEM(dims, F32)
 
-    return pl.pallas_call(
+    done = pl.pallas_call(
         kernel,
         out_shape=jax.ShapeDtypeStruct((5 * BS, 5 * BS), F32),
         in_specs=[SMEM, ANY, ANY],
@@ -505,27 +482,40 @@
             vmem(5 * BS, NPB * BS),
             vmem(NPB * BS, 5 * BS),
         ]
-        + [vmem(5, BS, BS)] * 6
+        + [vmem(5, BS, BS)] * 4
+        + [vmem(BS, BS), vmem(NPB, 2, 5, 8, BS), vmem(NPB, 2, 5, 8, BS)]
         + [
             dma((3,)),
-            dma((2, 5)),
-            dma((2, 5)),
-            dma((NPB, 5, 3)),
-            dma((NPB, 5)),
-            dma((NPB, 5, 4)),
-            dma((NPB, 5)),
+            dma((2,)),
+            dma((2, 16)),
+            dma((16,)),
+            dma((NPB, 2)),
+            dma((NPB, 2)),
+            dma((8,)),
+            dma((8,)),
+            dma((4,)),
+            dma((4,)),
+            dma((4,)),
+            dma((4,)),
+            dma((1,)),
+            dma((1,)),
             dma((15,)),
             dma((NPB, NPB, 4)),
             dma((NPB, NPB, 4)),
             dma((NPB, NPB)),
             dma((NPB, NPB)),
             dma((NPB, NPB)),
-            dma((PIECES,)),
-            dma((PIECES,)),
+            dma((2, 3)),
+            dma((2, 3)),
         ],
         compiler_params=pltpu.CompilerParams(collective_id=0, has_side_effects=True),
         name="front",
     )(child_maps, front, children)
+    s, r, q = position()
+    section = 8 * s + r
+    row = lax.broadcasted_iota(jnp.int32, done.shape, 0)
+    column = lax.broadcasted_iota(jnp.int32, done.shape, 1)
+    return jnp.where((section < NPB) & (row < BS) & (column // BS * 16 + q > section), 0.0, done)
 
 
 def solution(mesh):

time: 75.2 us -> 68.5 us (0.911)
  the two profiles are of different devices: /device:TPU:80 before, /device:TPU:137 now
where the time goes in v5:
time: 68.5 us; the launch traced here: 68.3 us
  Pallas kernels  65.5 us (96%)
  other arithmetic  2.85 us (4%)
    pallas_call x1, Pallas kernels, body(): pl.pallas_call(kernel, out_shape=jax.ShapeDtypeStruct((5 * BS, 5 * BS), F...  65.5 us
    select_n x1, other arithmetic, body(): jnp.where((section < NPB) & (row < BS) & (column // BS * 16 + q > section...  2.83 us

profile of v5, /device:TPU:137, one launch (start us, length us, event | category | flops | bytes accessed | tf_op | source)
XLA Modules:
  0.0 68.3 jit_solution(392482655879050884)
XLA Ops:
  0.0 65.5 %front.2 = f32[640,640]{1,0:T(8,128)} custom-call(s32[4,48]{1,0:T(4,128)} %maps.1, f32[640,640]{1,0:T(8,128)} %front.3, f32[2,768,384]{2,1,0:T(8,128)} %children.1), custom_call_target="tpu_custom_call" | custom-call | tf_op jit(solution)/shard_map/front/pallas_call | solution.py:467
  65.5 2.8 %fusion.1 = f32[640,640]{1,0:T(8,128)} fusion(f32[640,640]{1,0:T(8,128)} %front.2, s32[]{:T(128)S(6)} %add.11, s32[]{:T(128)S(6)} %axis_index.38, s32[640]{0:T(1024)S(1)} %get-tuple-element.5, s32[640]{0:T(1024)S(1)} %get-tuple-element.6, pred[640]{0:T(1024)(128)(4,1)S(1)} %get-tuple-element.7, pred[640]{0:T(1024)(128)(4,1)S(1)} %get-tuple-element.8), kind=kLoop, calls=%fused_computation.2 | loop fusion | flops 2457600 | bytes 3283208 | tf_op jit(solution)/shard_map/jit(_where)/select_n | solution.py:518
  (2 shorter events, 0.0 us)

commit v6 on v5

--- a/solution.py
+++ b/solution.py
@@ -8,6 +8,7 @@
 BS = 128
 NPB = 3
 LEAF = 8
+SUM_AFTER = 1
 Y_AT = (0, 4)
 Z_AT = (1, 4)
 F32 = jnp.float32
@@ -22,6 +23,18 @@
 
 def position():
     return lax.axis_index("sub"), lax.axis_index("row"), lax.axis_index("col")
+
+
+def split(a):
+    high = a.astype(jnp.bfloat16)
+    return high, (a - high.astype(F32)).astype(jnp.bfloat16)
+
+
+def dot3(a, b, dims):
+    def part(u, v):
+        return lax.dot_general(u, v, (dims, ((), ())), preferred_element_type=F32)
+
+    return part(a[0], b[0]) + (part(a[0], b[1]) + part(a[1], b[0]))
 
 
 def dot(a, b, dims):
@@ -282,8 +295,8 @@
         here = left.at[:, :, span(core, HALF)]
         act(copy(here, here, bs.at[0], br.at[0], sibling))
 
-    def pieces(act):
-        for c in range(2):
+    def pieces(act, children_at=range(2)):
+        for c in children_at:
             for u in range(3):
                 act(copy(kids.at[c, span(2 * u + 1 - s, BS), :], arrived.at[c, u], ps.at[c, u], pq.at[c, u], partner))
 
@@ -360,10 +373,18 @@
             corner_step(i, k, stage)
         if stage == 0:
             scatter(lambda c: c.start())
-    gather_sum()
-    along_x(lambda c: c.start())
-    along_z(lambda c: c.start())
-    pieces(lambda c: c.start())
+
+        if stage < 2:
+
+            @pl.when(((s == 0) & (r < NPB)) == (stage == 1))
+            def _():
+                pieces(lambda c: c.start(), [0])
+
+        if stage == SUM_AFTER:
+            gather_sum()
+            along_x(lambda c: c.start())
+            along_z(lambda c: c.start())
+            pieces(lambda c: c.start(), [1])
     for i, k in corners:
         other = corner.at[i, k, span(1 - core, HALF), :]
 
@@ -408,21 +429,28 @@
     along_y(lambda c: c.wait_recv())
     to_sibling(lambda c: c.wait_recv())
 
+    columns, rows = [], [[] for _ in range(5)]
+    low = {(k, i): split(lows[k, i]) for k in range(NPB) for i in range(k)}
     for k in range(NPB):
-        inv = inverses[k]
+        inv = split(inverses[k])
         own = left[k].reshape(5 * BS, BS)
         for i in range(k):
-            own = own - dot(panel[:, i * BS : (i + 1) * BS], lows[k, i], ROWS_T)
-        panel[:, k * BS : (k + 1) * BS] = dot(own, inv, ROWS_T)
+            own = own - dot3(columns[i], low[k, i], ROWS_T)
+        own = dot3(split(own), inv, ROWS_T)
+        panel[:, k * BS : (k + 1) * BS] = own
+        columns.append(split(own))
         for n in range(5):
             other = right[k, n]
             for i in range(k):
-                other = other - dot(lows[k, i], pr[i * BS : (i + 1) * BS, n * BS : (n + 1) * BS], PLAIN)
-            pr[k * BS : (k + 1) * BS, n * BS : (n + 1) * BS] = dot(inv, other, PLAIN)
-
+                other = other - dot3(low[k, i], rows[n][i], PLAIN)
+            other = dot3(inv, split(other), PLAIN)
+            pr[k * BS : (k + 1) * BS, n * BS : (n + 1) * BS] = other
+            rows[n].append(split(other))
+
+    across = split(pr[...])
     for a in range(5):
-        rows = slice(a * BS, (a + 1) * BS)
-        out[rows, :] = out[rows, :] - dot(panel[rows, :], pr[...], PLAIN)
+        strip = slice(a * BS, (a + 1) * BS)
+        out[strip, :] = out[strip, :] - dot3(split(panel[strip, :]), across, PLAIN)
 
     pieces(lambda c: c.wait())
 

time: 68.5 us -> 67 us (0.978)
  the two profiles are of different devices: /device:TPU:137 before, /device:TPU:226 now
where the time goes in v6:
time: 67 us; the launch traced here: 66.8 us
  Pallas kernels  64 us (96%)
  other arithmetic  2.85 us (4%)
    pallas_call x1, Pallas kernels, body(): pl.pallas_call(kernel, out_shape=jax.ShapeDtypeStruct((5 * BS, 5 * BS), F...  64 us
    select_n x1, other arithmetic, body(): jnp.where((section < NPB) & (row < BS) & (column // BS * 16 + q > section...  2.83 us

profile of v6, /device:TPU:226, one launch (start us, length us, event | category | flops | bytes accessed | tf_op | source)
XLA Modules:
  0.0 66.8 jit_solution(9111677191676998102)
XLA Ops:
  0.0 64.0 %front.2 = f32[640,640]{1,0:T(8,128)} custom-call(s32[4,48]{1,0:T(4,128)} %maps.1, f32[640,640]{1,0:T(8,128)} %front.3, f32[2,768,384]{2,1,0:T(8,128)} %children.1), custom_call_target="tpu_custom_call" | custom-call | tf_op jit(solution)/shard_map/front/pallas_call | solution.py:495
  64.0 2.8 %fusion.1 = f32[640,640]{1,0:T(8,128)} fusion(f32[640,640]{1,0:T(8,128)} %front.2, s32[]{:T(128)S(6)} %add.11, s32[]{:T(128)S(6)} %axis_index.38, s32[640]{0:T(1024)S(1)} %get-tuple-element.5, s32[640]{0:T(1024)S(1)} %get-tuple-element.6, pred[640]{0:T(1024)(128)(4,1)S(1)} %get-tuple-element.7, pred[640]{0:T(1024)(128)(4,1)S(1)} %get-tuple-element.8), kind=kLoop, calls=%fused_computation.2 | loop fusion | flops 2457600 | bytes 3283208 | tf_op jit(solution)/shard_map/jit(_where)/select_n | solution.py:546
  (2 shorter events, 0.0 us)

commit v7 on v6

--- a/solution.py
+++ b/solution.py
@@ -9,7 +9,6 @@
 NPB = 3
 LEAF = 8
 SUM_AFTER = 1
-Y_AT = (0, 4)
 Z_AT = (1, 4)
 F32 = jnp.float32
 MESH = pl.DeviceIdType.MESH
@@ -385,6 +384,8 @@
             along_x(lambda c: c.start())
             along_z(lambda c: c.start())
             pieces(lambda c: c.start(), [1])
+    along_x(lambda c: c.wait_recv())
+    along_y(lambda c: c.start())
     for i, k in corners:
         other = corner.at[i, k, span(1 - core, HALF), :]
 
@@ -397,13 +398,6 @@
     @pl.loop(0, NPB)
     def _(k):
         def after(t):
-            if t == Y_AT[1]:
-
-                @pl.when(k == Y_AT[0])
-                def _():
-                    along_x(lambda c: c.wait_recv())
-                    along_y(lambda c: c.start())
-
             if t == Z_AT[1]:
 
                 @pl.when(k == Z_AT[0])
@@ -484,6 +478,14 @@
         act(lambda c: c.wait_send())
     for i, k in corners:
         corner_sends(i, k, lambda c: c.wait_send())
+
+
+def clear_kernel(done, out):
+    s, r, q = position()
+    section = 8 * s + r
+    column = lax.broadcasted_iota(jnp.int32, done.shape, 1) // BS * 16 + q
+    pivot = (pl.program_id(0) == 0) & (section < NPB)
+    out[...] = jnp.where(pivot & (column > section), 0.0, done[...])
 
 
 def body(front, children, child_maps):
@@ -539,11 +541,15 @@
         compiler_params=pltpu.CompilerParams(collective_id=0, has_side_effects=True),
         name="front",
     )(child_maps, front, children)
-    s, r, q = position()
-    section = 8 * s + r
-    row = lax.broadcasted_iota(jnp.int32, done.shape, 0)
-    column = lax.broadcasted_iota(jnp.int32, done.shape, 1)
-    return jnp.where((section < NPB) & (row < BS) & (column // BS * 16 + q > section), 0.0, done)
+    strip = pl.BlockSpec((BS, 5 * BS), lambda i: (i, 0))
+    return pl.pallas_call(
+        clear_kernel,
+        grid=(5,),
+        out_shape=jax.ShapeDtypeStruct(done.shape, F32),
+        in_specs=[strip],
+        out_specs=strip,
+        name="clear",
+    )(done)
 
 
 def solution(mesh):

time: 67 us -> 69 us (1.030)
  the two profiles are of different devices: /device:TPU:226 before, /device:TPU:234 now
where the time goes in v7:
time: 69 us; the launch traced here: 68.8 us
  Pallas kernels  68.8 us (100%)
    pallas_call x1, Pallas kernels, body(): pl.pallas_call(kernel, out_shape=jax.ShapeDtypeStruct((5 * BS, 5 * BS), F...  64.7 us
    pallas_call x1, Pallas kernels, body(): pl.pallas_call(clear_kernel, grid=(5,), out_shape=jax.ShapeDtypeStruct(do...  4.16 us

profile of v7, /device:TPU:234, one launch (start us, length us, event | category | flops | bytes accessed | tf_op | source)
XLA Modules:
  0.0 68.8 jit_solution(16466099511667758544)
XLA Ops:
  0.0 64.7 %front.2.done = f32[640,640]{1,0:T(8,128)} custom-call(s32[4,48]{1,0:T(4,128)} %maps.1, f32[640,640]{1,0:T(8,128)} %front.3, f32[2,768,384]{2,1,0:T(8,128)} %children.1), custom_call_target="tpu_custom_call" | custom-call | tf_op jit(solution)/shard_map/front/pallas_call | solution.py:497
  64.7 4.2 %clear.1 = f32[640,640]{1,0:T(8,128)} custom-call(f32[640,640]{1,0:T(8,128)} %front.2.done), custom_call_target="tpu_custom_call" | custom-call | tf_op jit(solution)/shard_map/clear/pallas_call | solution.py:545
